TPU v7x, 256 devices: a whole 4x4x8 slice. The times are simulated.
256 devices in a mesh: tm: 16 (over y, x_hi, core), group: 16 (over z, x_lo).
Axes of the slice: x: 4 (x_hi: 2, x_lo: 2; x = x_hi * 2 + x_lo), y: 4, z: 8, core: 2. Of those that a mesh axis runs over, the one named last changes fastest.
Arguments:
- clips: bfloat16 [16, 128, 128, 512], P('group', 'tm'), may hold values from -6 to 6
- lengths: int32 [16, 8], P('group'), may hold values from 1 to 32, 128 in all within a row
- w_time: bfloat16 [3, 512, 512], P(None, 'tm'), may hold values from -0.15625 to 0.15625
- w_down: bfloat16 [3, 512, 512], P(None, 'tm'), may hold values from -0.15625 to 0.15625
- cotangent: bfloat16 [16, 64, 128, 512], P('group', 'tm'), may hold values from -6 to 6
Outputs:
- reduced: bfloat16 [16, 64, 128, 512], P('group', 'tm')
- grad_clips: bfloat16 [16, 128, 128, 512], P('group', 'tm')
- grad_time: float32 [3, 512, 512], P(None, 'tm')
- grad_down: float32 [3, 512, 512], P(None, 'tm')
All inputs are finite; a program needn't handle non-finite values.
Results may differ from a plain program's by a relative error of at most 0.0052.
Values may be sent and summed in bfloat16 or wider, within the bound.
A program may use at most 64 MiB of HBM per device.

v0:
```python
import jax
import jax.numpy as jnp
from jax import lax
from jax.sharding import PartitionSpec as P


def shifted(block, axis, distance):
    devices = range(lax.axis_size(axis))
    route = [(i - distance, i) for i in devices if i - distance in devices]
    return lax.ppermute(block, axis, route)


def clip_start(lengths_row, frames):
    ends = jnp.cumsum(lengths_row)
    return jnp.sum(jnp.where(ends[None, :] <= frames[:, None], lengths_row[None, :], 0), axis=1)


def features(x_wide):
    scale = lax.rsqrt(jnp.mean(x_wide * x_wide, axis=-1, keepdims=True) + 1e-06)
    return jax.nn.silu(x_wide * scale)


def project(block, weight):
    shape = block.shape
    flat = jnp.dot(block.reshape(-1, shape[-1]), weight, preferred_element_type=jnp.float32)
    return flat.reshape(shape[:-1] + (weight.shape[1],))


def outer(left, right):
    width = left.shape[-1]
    return jnp.dot(
        left.reshape(-1, width).T,
        right.reshape(-1, right.shape[-1]),
        preferred_element_type=jnp.float32,
    )


def shards(clips, lengths, w_time, w_down, cotangent):
    x_bf = clips[0]
    lengths_row = lengths[0]
    cot_local = cotangent[0]
    frame_count = x_bf.shape[0]
    half_count = frame_count // 2
    position = lax.axis_index("tm")
    frames = position * frame_count + jnp.arange(frame_count, dtype=jnp.int32)
    starts = clip_start(lengths_row, frames)
    time_full = lax.all_gather(w_time, "tm", axis=1, tiled=True)
    x_wide = x_bf.astype(jnp.float32)
    h_in = features(x_wide).astype(jnp.bfloat16)
    before = shifted(h_in[frame_count - 2 :], "tm", 1)
    h_ext = jnp.concatenate([before, h_in], axis=0)
    mixed = x_wide
    time_taps = []
    for offset in range(3):
        valid = frames - offset >= starts
        tapped = jnp.where(
            valid[:, None, None],
            h_ext[2 - offset : 2 - offset + frame_count],
            jnp.zeros((), jnp.bfloat16),
        )
        time_taps.append(tapped)
        mixed = mixed + project(tapped, time_full[offset])
    hidden = mixed.astype(jnp.bfloat16)
    down_full = lax.all_gather(w_down, "tm", axis=1, tiled=True)
    out_frames = position * frame_count + 2 * jnp.arange(half_count, dtype=jnp.int32)
    out_starts = clip_start(lengths_row, out_frames)
    hidden_before = shifted(hidden[frame_count - 2 :], "tm", 1)
    hidden_ext = jnp.concatenate([hidden_before, hidden], axis=0)
    reduced = jnp.zeros((half_count,) + hidden.shape[1:], jnp.float32)
    down_taps = []
    for offset in range(3):
        valid = out_frames - offset >= out_starts
        tapped = jnp.where(
            valid[:, None, None],
            hidden_ext[2 - offset : 2 - offset + frame_count][::2],
            jnp.zeros((), jnp.bfloat16),
        )
        down_taps.append(tapped)
        reduced = reduced + project(tapped, down_full[offset])
    grad_down = jnp.stack([outer(down_taps[offset], cot_local) for offset in range(3)])
    cot_next = shifted(cot_local[:1], "tm", -1)
    cot_ext = jnp.concatenate([cot_local, cot_next], axis=0)
    ext_frames = position * frame_count + 2 * jnp.arange(half_count + 1, dtype=jnp.int32)
    ext_starts = clip_start(lengths_row, ext_frames)
    grad_hidden = jnp.zeros(x_wide.shape, jnp.float32)
    for offset in range(3):
        valid = ext_frames - offset >= ext_starts
        spread = jnp.where(
            valid[:, None, None], project(cot_ext, down_full[offset].T), jnp.zeros((), jnp.float32)
        )
        placed = jnp.stack([spread, jnp.zeros_like(spread)], axis=1).reshape(
            (frame_count + 2,) + spread.shape[1:]
        )
        grad_hidden = grad_hidden + placed[offset : offset + frame_count]
    grad_mixed = grad_hidden.astype(jnp.bfloat16)
    grad_time = jnp.stack([outer(time_taps[offset], grad_mixed) for offset in range(3)])
    grad_next = shifted(grad_mixed[:2], "tm", -1)
    grad_ext = jnp.concatenate([grad_mixed, grad_next], axis=0)
    grad_hin = jnp.zeros(x_wide.shape, jnp.float32)
    for offset in range(3):
        valid = frames >= clip_start(lengths_row, frames + offset)
        tapped = jnp.where(
            valid[:, None, None],
            grad_ext[offset : offset + frame_count],
            jnp.zeros((), jnp.bfloat16),
        )
        grad_hin = grad_hin + project(tapped, time_full[offset].T)
    _, pullback = jax.vjp(features, x_wide)
    grad_feat = pullback(grad_hin)[0]
    grad_clips = (grad_hidden + grad_feat).astype(jnp.bfloat16)
    share_time, share_down = (
        lax.psum_scatter(grad_time, "tm", scatter_dimension=1, tiled=True),
        lax.psum_scatter(grad_down, "tm", scatter_dimension=1, tiled=True),
    )
    final_time, final_down = lax.psum((share_time, share_down), "group")
    return (reduced.astype(jnp.bfloat16)[None], grad_clips[None], final_time, final_down)


def solution(mesh):
    in_specs = (
        P("group", "tm", None, None),
        P("group", None),
        P(None, "tm", None),
        P(None, "tm", None),
        P("group", "tm", None, None),
    )
    out_specs = (
        P("group", "tm", None, None),
        P("group", "tm", None, None),
        P(None, "tm", None),
        P(None, "tm", None),
    )
    return jax.shard_map(shards, mesh=mesh, in_specs=in_specs, out_specs=out_specs, check_vma=False)
```

profile of v0, /device:TPU:2, one launch (start us, length us, event | category | flops | bytes accessed | tf_op | source)
XLA Modules:
  0.0 456.3 jit_solution(16601513061316640152)
XLA Ops:
  7.2 0.0 all-gather.5.cloned.1.call-start
  7.2 0.7 all-gather.5.cloned.1.call-update
  7.9 0.0 all-gather.3.cloned.1.call-start
  7.9 0.9 slice_bitcast_fusion.18
  8.9 1.3 collective-permute-start.2
  10.2 0.0 all-gather.3.cloned.1.call-update
  10.2 0.0 reduce-scatter.3.cloned.1.call-start
  10.3 0.8 reduce-window.8
  11.1 0.8 select_reduce_fusion.2
  11.9 0.9 select_reduce_fusion
  12.8 1.5 fusion.20
  14.4 49.7 %all-gather.5.cloned.1.call-done = bf16[3,512,512]{2,1,0:T(8,128)(2,1)} async-done(((bf16[3,32,512]{2,1,0:T(8,128)(2,1)}), bf16[3,512,512]{2,1,0:T(8,128)(2,1)}) %all-gather.5.cloned.1.call-update) | async-done | bytes 1572880 | tf_op jit(solution)/shard_map/all_gather | solution.py:64
  64.1 1.7 fusion.30
  65.8 0.2 pad_slice_fusion.1
  66.1 0.2 copy.15
  66.3 0.8 copy-done.5
  67.1 0.5 copy-done.11
  67.7 0.5 fusion.28
  68.2 0.2 pad_slice_fusion
  68.5 0.2 copy.17
  68.7 0.5 fusion.29
  69.2 0.3 stack.45.clone
  69.6 0.4 copy-done
  70.0 0.8 fusion.85
  70.8 0.4 copy-done.2
  71.3 1.3 collective-permute-start.3
  72.6 44.4 %all-gather.3.cloned.1.call-done = bf16[3,512,512]{2,1,0:T(8,128)(2,1)} async-done(((bf16[3,32,512]{2,1,0:T(8,128)(2,1)}), bf16[3,512,512]{2,1,0:T(8,128)(2,1)}) %all-gather.3.cloned.1.call-update) | async-done | bytes 1572880 | tf_op jit(solution)/shard_map/all_gather | solution.py:47
  117.0 1.9 fusion.50
  119.0 2.1 fusion.35
  121.1 2.8 fusion.24
  124.0 2.3 fusion.40
  126.3 2.2 collective-permute-start
  128.5 0.8 convolution_bitcast_fusion.5
  129.3 0.3 collective-permute-done
  129.7 0.8 convolution_bitcast_fusion.4
  130.5 0.8 convolution_bitcast_fusion.3
  131.3 1.9 pad_maximum_fusion
  133.2 0.0 reduce-scatter.5.cloned.1.call-start
  133.3 0.6 copy-done.14
  133.9 0.2 select_reduce_fusion.4
  134.1 0.6 copy-done.13
  134.6 1.0 fusion.43
  135.7 0.2 copy-done.8
  135.9 0.8 fusion.64
  136.6 0.9 fusion.23
  137.5 5.3 %collective-permute-start.1 = (bf16[2,128,512]{2,1,0:T(8,128)(2,1)S(1)}, bf16[2,128,512]{2,1,0:T(8,128)(2,1)S(1)}, u32[]{:S(2)}, u32[]{:S(2)}) collective-permute-start(bf16[2,128,512]{2,1,0:T(8,128)(2,1)S(1)} %slice.113), channel_id=1, source_target_pairs={{0,16},{16,32},{32,48},{48,64},{64,80},{80,96},{96,112},{112,128},... | collective-permute-start | bytes 786440 | tf_op jit(solution)/shard_map/ppermute | solution.py:10
  142.9 0.1 slice_select_fusion.2
  143.0 0.5 convolution_bitcast_fusion.2
  143.5 0.5 collective-permute-done.1
  144.0 0.1 pad_maximum_fusion.3
  144.2 0.1 slice_select_fusion
  144.3 0.5 convolution_bitcast_fusion
  144.7 0.1 slice_select_fusion.1
  144.8 0.5 convolution_bitcast_fusion.1
  145.3 2.0 pad_maximum_fusion.1
  147.3 0.0 all-reduce.6.cloned.1.call-start
  147.4 1.5 fusion.65
  148.8 72.5 %reduce-scatter.3.cloned.1.call-done = f32[3,32,512]{2,1,0:T(8,128)} async-done(((f32[3,512,512]{2,1,0:T(8,128)}), f32[3,32,512]{2,1,0:T(8,128)}) %reduce-scatter.3.cloned.1.call-update) | async-done | bytes 196624 | tf_op jit(solution)/shard_map/reduce_scatter | solution.py:112
  221.4 86.1 %reduce-scatter.5.cloned.1.call-done = f32[3,32,512]{2,1,0:T(8,128)} async-done(((f32[3,512,512]{2,1,0:T(8,128)}), f32[3,32,512]{2,1,0:T(8,128)}) %reduce-scatter.5.cloned.1.call-update) | async-done | bytes 196624 | tf_op jit(solution)/shard_map/reduce_scatter | solution.py:113
  307.5 1.5 convolution_add_fusion.1
  309.0 2.3 fusion.32
  311.2 135.3 %all-reduce.6.cloned.1.call-done = (f32[3,32,512]{2,1,0:T(8,128)}, f32[3,32,512]{2,1,0:T(8,128)}) async-done(((f32[3,32,512]{2,1,0:T(8,128)}, f32[3,32,512]{2,1,0:T(8,128)}), (f32[3,32,512]{2,1,0:T(8,128)}, f32[3,32,512]{2,1,0:T(8,128)})) %all-reduce.6.cloned.1.call-update) | async-done | bytes 393232 | tf_op jit(solution)/shard_map/psum | solution.py:115
  446.5 1.6 copy.27
  448.1 1.6 copy.28
  (42 shorter events, 0.2 us)
Async XLA Ops:
  7.2 56.9 %all-gather.5.cloned.1.call-start = ((), (), s32[]{:S(2)}) async-start(), calls=%async_computation.3 | async-start | bytes 1671168 | tf_op jit(solution)/shard_map/all_gather | solution.py:64
  7.9 109.1 %all-gather.3.cloned.1.call-start = ((), (), s32[]{:S(2)}) async-start(), calls=%async_computation.2 | async-start | bytes 1671168 | tf_op jit(solution)/shard_map/all_gather | solution.py:47
  8.9 5.5 %collective-permute-start.2 = (bf16[1,128,512]{2,1,0:T(8,128)(2,1)S(1)}, bf16[1,128,512]{2,1,0:T(8,128)(2,1)S(1)}, u32[]{:S(2)}, u32[]{:S(2)}) collective-permute-start(bf16[1,128,512]{2,1,0:T(8,128)(2,1)S(1)} %slice_bitcast_fusion.18), channel_id=1, source_target_pairs={{16,0},{32,16},{48,32},{64,48},{80,64},{96,80},{112,96},{128,112},... | collective-permute-start | bytes 393224 | tf_op jit(solution)/shard_map/ppermute | solution.py:10
  10.2 211.2 %reduce-scatter.3.cloned.1.call-start = ((), (), s32[]{:S(2)}) async-start(), calls=%async_computation.4 | async-start | bytes 3342336 | tf_op jit(solution)/shard_map/reduce_scatter | solution.py:112
  66.1 1.0 copy-start.5
  66.1 1.6 copy-start.11
  68.7 1.3 copy-start
  69.6 1.7 copy-start.2
  71.2 45.8 %copy-start.9 = (bf16[8,128,512]{2,1,0:T(8,128)(2,1)}, bf16[8,128,512]{2,1,0:T(8,128)(2,1)S(1)}, u32[]{:S(2)}) copy-start(bf16[8,128,512]{2,1,0:T(8,128)(2,1)S(1)} %fusion.85) | copy-start | bytes 3145732
  71.3 47.7 %collective-permute-start.3 = (bf16[2,128,512]{2,1,0:T(8,128)(2,1)S(1)}, bf16[2,128,512]{2,1,0:T(8,128)(2,1)}, u32[]{:S(2)}, u32[]{:S(2)}) collective-permute-start(bf16[2,128,512]{2,1,0:T(8,128)(2,1)S(1)} %slice.119), channel_id=1, source_target_pairs={{16,0},{32,16},{48,32},{64,48},{80,64},{96,80},{112,96},{128,112},... | collective-permute-start | bytes 786440 | tf_op jit(solution)/shard_map/ppermute | solution.py:10
  117.0 1.9 copy-start.12
  118.9 2.1 copy-start.4
  118.9 2.1 copy-start.10
  121.1 2.9 copy-start.1
  121.1 2.9 copy-start.3
  126.3 4.2 copy-start.7
  126.3 3.3 collective-permute-start
  133.2 0.7 copy-start.14
  133.2 1.4 copy-start.13
  133.2 174.2 %reduce-scatter.5.cloned.1.call-start = ((), (), s32[]{:S(2)}) async-start(), calls=%async_computation.5 | async-start | bytes 3342336 | tf_op jit(solution)/shard_map/reduce_scatter | solution.py:113
  134.6 1.2 copy-start.8
  136.6 6.4 %copy-start.6 = (bf16[1,4,128,512]{3,2,1,0:T(8,128)(2,1)S(1)}, bf16[1,4,128,512]{3,2,1,0:T(8,128)(2,1)}, u32[]{:S(2)}) copy-start(bf16[1,4,128,512]{3,2,1,0:T(8,128)(2,1)} %param.9) | copy-start | bytes 1572868
  137.5 6.5 %collective-permute-start.1 = (bf16[2,128,512]{2,1,0:T(8,128)(2,1)S(1)}, bf16[2,128,512]{2,1,0:T(8,128)(2,1)S(1)}, u32[]{:S(2)}, u32[]{:S(2)}) collective-permute-start(bf16[2,128,512]{2,1,0:T(8,128)(2,1)S(1)} %slice.113), channel_id=1, source_target_pairs={{0,16},{16,32},{32,48},{48,64},{64,80},{80,96},{96,112},{112,128},... | collective-permute-start | bytes 786440 | tf_op jit(solution)/shard_map/ppermute | solution.py:10
  147.3 299.2 %all-reduce.6.cloned.1.call-start = ((), (), s32[]{:S(2)}) async-start(), calls=%async_computation.6 | async-start | bytes 786432 | tf_op jit(solution)/shard_map/psum | solution.py:115
Sparse Core Ops, SparseCore 0:
  10.8 53.3 all-gather.4
  66.9 50.1 all-gather.2
  133.4 87.9 reduce-scatter.2
  225.6 81.8 reduce-scatter.4
  310.0 136.4 all-reduce.5
where the time goes:
time: 457 us; the launch traced here: 456 us
  waiting for transfers between devices  390 us (85%)
  matrix products  21.3 us (5%)
  between operations  14.2 us (3%)
  other arithmetic  11.9 us (3%)
  starting transfers between devices  10.3 us (2%)
  local copies, waits for them, and re-layouts  9 us (2%)
    psum x1, waiting for transfers between devices, shards(): final_time, final_down = lax.psum((share_time, share_down), 'group')  135 us
    reduce_scatter x1, waiting for transfers between devices, shards(): lax.psum_scatter(grad_down, 'tm', scatter_dimension=1, tiled=True)  86.1 us
    reduce_scatter x1, waiting for transfers between devices, shards(): lax.psum_scatter(grad_time, 'tm', scatter_dimension=1, tiled=True)  72.5 us
    all_gather x1, waiting for transfers between devices, shards(): down_full = lax.all_gather(w_down, 'tm', axis=1, tiled=True)  49.7 us
    all_gather x1, waiting for transfers between devices, shards(): time_full = lax.all_gather(w_time, 'tm', axis=1, tiled=True)  44.4 us
    dot_general x12, matrix products, project(): jnp.dot(block.reshape(-1, shape[-1]), weight, preferred_element_type=jnp....  17.5 us
    ppermute x4, starting transfers between devices, shifted(): return lax.ppermute(block, axis, route)  10.1 us
  transfers between devices with their start and end apart: 9, of which 7 were waited for; matrix products, arithmetic and copies ran while one was open for 5% of the time, Pallas kernels for 0%

commit v1 on v0

v1 whole, which is shorter than its diff:
```python
import functools

import jax
import jax.numpy as jnp
from jax import lax
from jax.experimental import pallas as pl
from jax.experimental.pallas import tpu as pltpu
from jax.sharding import PartitionSpec as P

MESH = pl.DeviceIdType.MESH
BF = jnp.bfloat16
F32 = jnp.float32
FD, HD, S, C, NC = 8, 4, 128, 512, 8
NT = 16
NZ = 8
EPS = 1e-06


def dot(a, b, ca, cb):
    return lax.dot_general(a, b, (((ca,), (cb,)), ((), ())), preferred_element_type=F32)


def device(x, y, z, core):
    return {"tm": y * 4 + (x // 2) * 2 + core, "group": z * 2 + x % 2}


def kernel(
    lengths,
    clips,
    wt_own,
    wd_own,
    cot,
    reduced,
    grad_clips,
    pieces,
    wt,
    wd,
    clips_halo,
    cot_ext,
    h_ext,
    taps,
    gh,
    gm,
    hid,
    dtaps,
    gtap,
    stage,
    acc,
    core_out,
    core_in,
    out1,
    in1,
    out2,
    in2,
    out3,
    in3,
    out4,
    in4,
    z_out,
    z_in,
    piece,
    w_send,
    w_recv,
    halo_send,
    halo_recv,
    core_send,
    core_recv,
    ring_send,
    ring_recv,
    z_send,
    z_recv,
    p_send,
    p_recv,
    l_sem,
):
    t = lax.axis_index("tm")
    group = lax.axis_index("group")
    y, xh, c = t // 4, (t // 2) % 2, t % 2
    z, xl = group // 2, group % 2
    x = 2 * xh + xl

    def at(dx, dy, dz, dc):
        return device((x + dx + 4) % 4, (y + dy + 4) % 4, (z + dz + NZ) % NZ, (c + dc) % 2)

    sibling = at(0, 0, 0, 1)
    up, down = at(0, 1, 0, 0), at(0, -1, 0, 0)
    mirror = device(3 - x, y, z, c)
    step = 2 * c - 1
    far = {"tm": (t + step + NT) % NT, "group": group}

    def remote(src, dst, send, recv, target):
        return pltpu.make_async_remote_copy(
            src_ref=src,
            dst_ref=dst,
            send_sem=send,
            recv_sem=recv,
            device_id=target,
            device_id_type=MESH,
        )

    barrier = pltpu.get_barrier_semaphore()
    peers = [sibling, up, down, at(1, 0, 0, 0), at(-1, 0, 0, 0), far]
    peers += [at(0, 0, d, 0) for d in range(1, NZ)]
    mate = 1 - 2 * xl
    peers += [at(mate, 0, d, 0) for d in range(1, NZ)]
    for peer in peers:
        pl.semaphore_signal(barrier, inc=1, device_id=peer, device_id_type=MESH)
    pl.semaphore_wait(barrier, len(peers))

    def clips_copy(target):
        return remote(
            clips.at[pl.ds(FD - 4, 4)], clips_halo, halo_send.at[0], halo_recv.at[0], target
        )

    def cot_copy(target):
        return remote(
            cot.at[pl.ds(0, 2)], cot_ext.at[pl.ds(HD, 2)], halo_send.at[1], halo_recv.at[1], target
        )

    after = {"tm": (t + 1) % NT, "group": group}
    before = {"tm": (t + NT - 1) % NT, "group": group}

    def rows(ref, owner):
        return ref.at[:, pl.ds(pl.multiple_of(owner * 32, 32), 32), :]

    def owner_of(dy, other):
        h = 1 - xh if other else xh
        return ((y + dy + 4) % 4) * 4 + h * 2 + c

    blocks = [(0, 1), (-1, 0), (1, 0), (-1, 1), (1, 1), (2, 0), (2, 1)]

    def block_send(w, number, src, owner, to, slot):
        full = (wd, wt)[w]
        return remote(
            rows(full, owner) if src is None else src,
            rows(full, owner),
            w_send.at[w, number],
            w_recv.at[w, slot],
            to,
        )

    def first_sends(w):
        own = (wd_own, wt_own)[w]
        return [
            block_send(w, 0, own, t, up, 1),
            block_send(w, 1, own, t, down, 2),
            block_send(w, 2, own, t, mirror, 0),
            block_send(w, 3, own, t, sibling, 7),
        ]

    def passes(w, index):
        owner = owner_of(*blocks[index])
        sends = [block_send(w, 4 + index, None, owner, sibling, 8 + index)]
        if index == 0:
            sends = [
                block_send(w, 11, None, owner, up, 3),
                block_send(w, 12, None, owner, down, 4),
            ] + sends
        if index == 1:
            sends = [block_send(w, 13, None, owner, up, 5)] + sends
        if index == 4:
            sends = [block_send(w, 14, None, owner, down, 6)] + sends
        return sends

    def own_copy(w):
        return pltpu.make_async_copy(
            (wd_own, wt_own)[w], rows((wd, wt)[w], t), l_sem.at[w]
        )

    def arrive(w, index):
        owner = owner_of(*blocks[index])
        block_send(w, 4 + index, None, owner, sibling, index).wait_recv()
        for copy in passes(w, index):
            copy.start()

    def finish_weights(w):
        own_copy(w).wait()
        full = (wd, wt)[w]
        for slot in range(7, 15):
            other = t + 1 - 2 * c if slot == 7 else owner_of(*blocks[slot - 8]) + 1 - 2 * c
            block_send(w, 0, None, other, sibling, slot).wait_recv()

    for copy in first_sends(0):
        copy.start()
    own_copy(0).start()
    own_copy(1).start()

    @pl.when(t > 0)
    def _():
        cot_copy(before).start()

    @pl.when(t < NT - 1)
    def _():
        clips_copy(after).start()

    def length(i):
        return lengths[0, i]

    ends = [length(0)]
    for i in range(1, NC):
        ends.append(ends[-1] + length(i))
    first = t * FD

    def opens(frame):
        f = first + frame
        hit = f == 0
        for end in ends:
            hit = jnp.logical_or(hit, f == end)
        return hit

    opening = {i: opens(i) for i in range(-3, 11)}

    def live(k, frame):
        if k == 0:
            return None
        out = jnp.logical_not(opening[frame])
        if k == 2:
            out = jnp.logical_and(out, jnp.logical_not(opening[frame - 1]))
        return out

    def masked(keep, value):
        return value if keep is None else jnp.where(keep, value, jnp.zeros_like(value))

    def features(block):
        wide = block.astype(F32)
        scale = lax.rsqrt(jnp.mean(wide * wide, axis=-1, keepdims=True) + EPS)
        v = wide * scale
        return (v / (1.0 + jnp.exp(-v))).astype(BF)

    def feature_body(i, _):
        h_ext[4 + i] = features(clips[i])
        return 0

    cot_ext[pl.ds(0, HD)] = cot[...]
    lax.fori_loop(0, FD // 2, feature_body, 0)
    arrive(0, 0)
    lax.fori_loop(FD // 2, FD, feature_body, 0)
    arrive(0, 1)
    arrive(0, 2)
    for copy in first_sends(1):
        copy.start()
    arrive(0, 3)
    arrive(0, 4)
    arrive(0, 5)
    arrive(0, 6)

    @pl.when(t < NT - 1)
    def _():
        cot_copy(before).wait_recv()

    @pl.when(t == NT - 1)
    def _():
        cot_ext[pl.ds(HD, 2)] = jnp.zeros((2, S, C), BF)

    finish_weights(0)

    flat0 = cot_ext[pl.ds(0, 5)].reshape(5 * S, C)
    flat1 = cot_ext[pl.ds(1, 5)].reshape(5 * S, C)
    p0 = dot(flat0, wd[0], 1, 1).reshape(5, S, C)
    for j in range(5):
        gh[2 * j] = p0[j]
    p2 = dot(flat1, wd[2], 1, 1).reshape(5, S, C)
    for j in range(5):
        total = gh[2 * j] + masked(live(2, 2 * j + 2), p2[j])
        gh[2 * j] = total
        gm[2 * j] = total.astype(BF)
    p1 = dot(flat1, wd[1], 1, 1).reshape(5, S, C)
    for j in range(5):
        total = masked(live(1, 2 * j + 2), p1[j])
        gh[2 * j + 1] = total
        gm[2 * j + 1] = total.astype(BF)

    arrive(1, 0)
    arrive(1, 1)
    arrive(1, 2)

    @pl.when(t > 0)
    def _():
        clips_copy(after).wait_recv()

    @pl.when(t == 0)
    def _():
        clips_halo[...] = jnp.zeros((4, S, C), BF)

    def halo_body(i, _):
        h_ext[i] = features(clips_halo[i])
        return 0

    lax.fori_loop(0, 4, halo_body, 0)
    for k in range(3):
        for i in range(10):
            taps[k, i] = masked(live(k, i - 2), h_ext[i + 2 - k])

    def core_copy(g, k):
        return remote(
            core_out.at[g, k], core_in.at[g, k], core_send.at[g, k], core_recv.at[g, k], sibling
        )

    def contribute(g, k, value):
        stage[g] = value.reshape(4, 2, 2, 2, 16, C)
        for yy in range(4):
            for h in range(2):
                for l in range(2):
                    acc[g, k, 2 * h + l, yy] = stage[g, yy, h, c, l]
                    core_out[g, k, 2 * h + l, yy] = stage[g, yy, h, 1 - c, l].astype(BF)
        core_copy(g, k).start()

    def merge(g):
        for k in range(3):
            core_copy(g, k).wait_recv()
            acc[g, k] = acc[g, k] + core_in[g, k].astype(F32)

    def neighbours(along_x):
        if along_x:
            return x, at(1, 0, 0, 0), at(-1, 0, 0, 0)
        return y, up, down

    def outer_block(g, index):
        return acc.at[g, :, index] if g == 0 else acc.at[g, :, :, index]

    def inner_block(g, index):
        return acc.at[g, :, x, index] if g == 0 else acc.at[g, :, index, y]

    def ring_copy(g, stage_no, side, target):
        src = (out1, out2, out3, out4)[stage_no].at[g, side]
        dst = (in1, in2, in3, in4)[stage_no].at[g, side]
        return remote(
            src,
            dst,
            ring_send.at[g, stage_no, side],
            ring_recv.at[g, stage_no, side],
            target,
        )

    def ring_recv_wait(g, stage_no, side, target):
        ring_copy(g, stage_no, side, target).wait_recv()

    def outer1(g):
        at_, plus, minus = neighbours(g == 0)
        block = outer_block(g, (at_ + 2) % 4)
        out1[g, 0] = block[:, pl.ds(0, 2)].astype(BF)
        ring_copy(g, 0, 0, plus).start()
        out1[g, 1] = block[:, pl.ds(2, 2)].astype(BF)
        ring_copy(g, 0, 1, minus).start()

    def outer2(g):
        at_, plus, minus = neighbours(g == 0)
        block = outer_block(g, (at_ + 1) % 4)
        ring_recv_wait(g, 0, 0, plus)
        out2[g, 0, :, pl.ds(0, 2)] = (block[:, pl.ds(0, 2)] + in1[g, 0].astype(F32)).astype(BF)
        out2[g, 0, :, pl.ds(2, 2)] = block[:, pl.ds(2, 2)].astype(BF)
        ring_copy(g, 1, 0, plus).start()
        block = outer_block(g, (at_ + 3) % 4)
        ring_recv_wait(g, 0, 1, minus)
        out2[g, 1, :, pl.ds(2, 2)] = (block[:, pl.ds(2, 2)] + in1[g, 1].astype(F32)).astype(BF)
        out2[g, 1, :, pl.ds(0, 2)] = block[:, pl.ds(0, 2)].astype(BF)
        ring_copy(g, 1, 1, minus).start()

    def outer3(g):
        at_, plus, minus = neighbours(g == 0)
        ring_recv_wait(g, 1, 0, plus)
        ring_recv_wait(g, 1, 1, minus)
        block = outer_block(g, at_)
        block[...] = block[...] + in2[g, 0].astype(F32) + in2[g, 1].astype(F32)

    def inner1(g):
        at_, plus, minus = neighbours(g == 1)
        block = inner_block(g, (at_ + 2) % 4)
        out3[g, 0] = block[:, :, pl.ds(0, 256)].astype(BF)
        ring_copy(g, 2, 0, plus).start()
        out3[g, 1] = block[:, :, pl.ds(256, 256)].astype(BF)
        ring_copy(g, 2, 1, minus).start()

    def inner2(g):
        at_, plus, minus = neighbours(g == 1)
        block = inner_block(g, (at_ + 1) % 4)
        ring_recv_wait(g, 2, 0, plus)
        out4[g, 0, :, :, pl.ds(0, 256)] = (
            block[:, :, pl.ds(0, 256)] + in3[g, 0].astype(F32)
        ).astype(BF)
        out4[g, 0, :, :, pl.ds(256, 256)] = block[:, :, pl.ds(256, 256)].astype(BF)
        ring_copy(g, 3, 0, plus).start()
        block = inner_block(g, (at_ + 3) % 4)
        ring_recv_wait(g, 2, 1, minus)
        out4[g, 1, :, :, pl.ds(256, 256)] = (
            block[:, :, pl.ds(256, 256)] + in3[g, 1].astype(F32)
        ).astype(BF)
        out4[g, 1, :, :, pl.ds(0, 256)] = block[:, :, pl.ds(0, 256)].astype(BF)
        ring_copy(g, 3, 1, minus).start()

    def inner3(g):
        at_, plus, minus = neighbours(g == 1)
        ring_recv_wait(g, 3, 0, plus)
        ring_recv_wait(g, 3, 1, minus)
        block = acc.at[g, :, x, y]
        block[...] = block[...] + in4[g, 0].astype(F32) + in4[g, 1].astype(F32)

    def time_grad(k):
        left = taps[k, pl.ds(2, FD)].reshape(FD * S, C)
        contribute(0, k, dot(left, gm[pl.ds(0, FD)].reshape(FD * S, C), 0, 0))

    time_grad(0)
    arrive(1, 3)
    arrive(1, 4)
    time_grad(1)
    arrive(1, 5)
    arrive(1, 6)
    time_grad(2)
    for k in range(1, 3):
        for f in range(FD):
            gtap[k - 1, f] = masked(live(k, f + k), gm[f + k])
    finish_weights(1)

    def hidden_pair(i, wide):
        total = wide
        for k in range(3):
            total = total + dot(taps[k, pl.ds(i, 2)].reshape(2 * S, C), wt[k], 1, 0)
        hid[pl.ds(i, 2)] = total.astype(BF).reshape(2, S, C)

    hidden_pair(0, clips_halo[pl.ds(2, 2)].astype(F32).reshape(2 * S, C))

    def hidden_body(i, _):
        hidden_pair(2 + 2 * i, clips[pl.ds(2 * i, 2)].astype(F32).reshape(2 * S, C))
        return 0

    lax.fori_loop(0, FD // 2, hidden_body, 0)
    merge(0)
    outer1(0)
    for k in range(3):
        for j in range(HD):
            dtaps[k, j] = masked(live(k, 2 * j), hid[2 * j + 2 - k])

    def down_grad(k):
        contribute(1, k, dot(dtaps[k].reshape(HD * S, C), cot[...].reshape(HD * S, C), 0, 0))

    down_grad(0)
    down_grad(1)
    down_grad(2)
    outer2(0)
    total = dot(dtaps[0].reshape(HD * S, C), wd[0], 1, 0)
    total = total + dot(dtaps[1].reshape(HD * S, C), wd[1], 1, 0)
    total = total + dot(dtaps[2].reshape(HD * S, C), wd[2], 1, 0)
    reduced[...] = total.astype(BF).reshape(HD, S, C)
    merge(1)
    outer1(1)

    def clips_pair(i, _):
        here = pl.ds(2 * i, 2)
        g = dot(gm[here].reshape(2 * S, C), wt[0], 1, 1)
        g = g + dot(gtap[0, here].reshape(2 * S, C), wt[1], 1, 1)
        g = g + dot(gtap[1, here].reshape(2 * S, C), wt[2], 1, 1)
        wide = clips[here].astype(F32).reshape(2 * S, C)
        scale = lax.rsqrt(jnp.mean(wide * wide, axis=-1, keepdims=True) + EPS)
        v = wide * scale
        sig = 1.0 / (1.0 + jnp.exp(-v))
        d = g * (sig * (1.0 + v * (1.0 - sig)))
        inner = jnp.mean(d * v, axis=-1, keepdims=True)
        grad = (d - v * inner) * scale
        grad_clips[here] = (gh[here].reshape(2 * S, C) + grad).astype(BF).reshape(2, S, C)
        return 0

    lax.fori_loop(0, 1, clips_pair, 0)
    outer3(0)
    inner1(0)
    lax.fori_loop(1, 2, clips_pair, 0)
    outer2(1)
    lax.fori_loop(2, 3, clips_pair, 0)
    inner2(0)
    lax.fori_loop(3, 4, clips_pair, 0)
    inner3(0)
    outer3(1)
    inner1(1)
    inner2(1)
    inner3(1)

    def z_copy(d):
        return remote(
            z_out.at[d - 1], z_in.at[d - 1], z_send.at[d - 1], z_recv.at[d - 1], at(0, 0, d, 0)
        )

    for g in range(2):
        for q in range(4):
            z_out[8 + g * 4 + q] = acc[g, :, x, y, :, pl.ds(128 * q, 128)].astype(BF)
    for d in range(1, NZ):
        z_out[d - 1] = z_out[8 + (z + d) % NZ]
        z_copy(d).start()
    total = z_out[8 + z].astype(F32)
    for d in range(1, NZ):
        z_copy(d).wait_recv()
        total = total + z_in[d - 1].astype(F32)
    piece[...] = total.astype(BF)

    def piece_copy(other, d):
        number = other * NZ + d - 1
        return remote(
            piece, pieces.at[z, xl], p_send.at[number], p_recv.at[number], at(mate * other, 0, d, 0)
        )

    sends = [(1, d) for d in range(NZ)] + [(0, d) for d in range(1, NZ)]
    for other, d in sends:
        piece_copy(other, d).start()
    pieces[z, xl] = piece[...]
    for other, d in sends:
        piece_copy(other, d).wait()

    @pl.when(t > 0)
    def _():
        cot_copy(before).wait_send()

    @pl.when(t < NT - 1)
    def _():
        clips_copy(after).wait_send()

    for w in range(2):
        for copy in first_sends(w):
            copy.wait_send()
        for index in range(7):
            for copy in passes(w, index):
                copy.wait_send()
    for g in range(2):
        for k in range(3):
            core_copy(g, k).wait_send()
        for stage_no in range(4):
            _, plus, minus = neighbours((g == 0) == (stage_no < 2))
            ring_copy(g, stage_no, 0, plus).wait_send()
            ring_copy(g, stage_no, 1, minus).wait_send()
    for d in range(1, NZ):
        z_copy(d).wait_send()


def shards(clips, lengths, w_time, w_down, cotangent):
    vmem = pl.BlockSpec(memory_space=pltpu.VMEM)
    dma = pltpu.SemaphoreType.DMA
    reduced, grad_clips, pieces = pl.pallas_call(
        kernel,
        out_shape=(
            jax.ShapeDtypeStruct((HD, S, C), BF),
            jax.ShapeDtypeStruct((FD, S, C), BF),
            jax.ShapeDtypeStruct((NZ, 2, 3, 16, 128), BF),
        ),
        in_specs=[pl.BlockSpec(memory_space=pltpu.SMEM)] + [vmem] * 4,
        out_specs=(vmem, vmem, vmem),
        scratch_shapes=[
            pltpu.VMEM((3, C, C), BF),
            pltpu.VMEM((3, C, C), BF),
            pltpu.VMEM((4, S, C), BF),
            pltpu.VMEM((HD + 2, S, C), BF),
            pltpu.VMEM((FD + 4, S, C), BF),
            pltpu.VMEM((3, FD + 2, S, C), BF),
            pltpu.VMEM((FD + 2, S, C), F32),
            pltpu.VMEM((FD + 2, S, C), BF),
            pltpu.VMEM((FD + 2, S, C), BF),
            pltpu.VMEM((3, HD, S, C), BF),
            pltpu.VMEM((2, FD, S, C), BF),
            pltpu.VMEM((2, 4, 2, 2, 2, 16, C), F32),
            pltpu.VMEM((2, 3, 4, 4, 16, C), F32),
            pltpu.VMEM((2, 3, 4, 4, 16, C), BF),
            pltpu.VMEM((2, 3, 4, 4, 16, C), BF),
            pltpu.VMEM((2, 2, 3, 2, 16, C), BF),
            pltpu.VMEM((2, 2, 3, 2, 16, C), BF),
            pltpu.VMEM((2, 2, 3, 4, 16, C), BF),
            pltpu.VMEM((2, 2, 3, 4, 16, C), BF),
            pltpu.VMEM((2, 2, 3, 16, 256), BF),
            pltpu.VMEM((2, 2, 3, 16, 256), BF),
            pltpu.VMEM((2, 2, 3, 16, C), BF),
            pltpu.VMEM((2, 2, 3, 16, C), BF),
            pltpu.VMEM((2 * NZ, 3, 16, 128), BF),
            pltpu.VMEM((NZ - 1, 3, 16, 128), BF),
            pltpu.VMEM((3, 16, 128), BF),
            dma((2, 15)),
            dma((2, 15)),
            dma((2,)),
            dma((2,)),
            dma((2, 3)),
            dma((2, 3)),
            dma((2, 4, 2)),
            dma((2, 4, 2)),
            dma((NZ - 1,)),
            dma((NZ - 1,)),
            dma((2 * NZ,)),
            dma((2 * NZ,)),
            dma((2,)),
        ],
        name="clip_conv",
        compiler_params=pltpu.CompilerParams(
            collective_id=0, has_side_effects=True, vmem_limit_bytes=60 * 2**20
        ),
    )(lengths, clips[0], w_time, w_down, cotangent[0])
    grads = pieces.reshape(2, 4, 2, 3, 16, 128).transpose(0, 3, 2, 4, 1, 5)
    grads = grads.reshape(2, 3, 32, C).astype(F32)
    return reduced[None], grad_clips[None], grads[0], grads[1]


def solution(mesh):
    in_specs = (
        P("group", "tm", None, None),
        P("group", None),
        P(None, "tm", None),
        P(None, "tm", None),
        P("group", "tm", None, None),
    )
    out_specs = (
        P("group", "tm", None, None),
        P("group", "tm", None, None),
        P(None, "tm", None),
        P(None, "tm", None),
    )
    return jax.shard_map(shards, mesh=mesh, in_specs=in_specs, out_specs=out_specs, check_vma=False)
```

time: 457 us -> 93.8 us (0.21)
  waiting for transfers between devices: 390 us -> 0 us
  Pallas kernels: 0 us -> 88.5 us
  matrix products: 21.3 us -> 0 us
  between operations: 14.2 us -> 0.68 us
  other arithmetic: 11.9 us -> 0.96 us
  starting transfers between devices: 10.3 us -> 0 us
  local copies, waits for them, and re-layouts: 9 us -> 3.57 us
    reduce_scatter x2 -> x0, waiting for transfers between devices: 159 us -> none  [the longest x1 86.1 us: shards(): lax.psum_scatter(grad_down, 'tm', scatter_dimension=1, tiled=True)]
    psum x1 -> x0, waiting for transfers between devices: 135 us -> none  [shards(): final_time, final_down = lax.psum((share_time, share_down), 'group')]
    all_gather x2 -> x0, waiting for transfers between devices: 94.2 us -> none  [the longest x1 49.7 us: shards(): down_full = lax.all_gather(w_down, 'tm', axis=1, tiled=True)]
    pallas_call x0 -> x1, Pallas kernels: none -> 88.5 us  [shards(): pl.pallas_call(kernel, out_shape=(jax.ShapeDtypeStruct((HD, S, C), BF), j...]
    dot_general x18 -> x0, matrix products: 21.3 us -> none  [the longest x12 17.5 us: project(): jnp.dot(block.reshape(-1, shape[-1]), weight, preferred_element_type=jnp....]
    ppermute x4 -> x0, starting transfers between devices: 10.1 us -> none  [shifted(): return lax.ppermute(block, axis, route)]
    unnamed x32 -> x6, local copies, waits for them, and re-layouts: 6.86 us -> 1.77 us
    another operation x3 -> x0, other arithmetic: 4.75 us -> none  [the longest x1 1.99 us: shards(): jnp.stack([outer(down_taps[offset], cot_local) for offset in range(3)])]
  transfers between devices with their start and end apart: 9 -> 0, of which waited for: 7 -> 0; matrix products, arithmetic and copies ran while one was open for 5% -> 0% of each run, Pallas kernels for 0% -> 0%
where the time goes in v1:
time: 93.8 us; the launch traced here: 93.7 us
  Pallas kernels  88.5 us (94%)
  local copies, waits for them, and re-layouts  3.57 us (4%)
  other arithmetic  0.96 us (1%)
    pallas_call x1, Pallas kernels, shards(): pl.pallas_call(kernel, out_shape=(jax.ShapeDtypeStruct((HD, S, C), BF), j...  88.5 us

profile of v1, /device:TPU:2, one launch (start us, length us, event | category | flops | bytes accessed | tf_op | source)
XLA Modules:
  0.0 93.7 jit_solution(2986280201593747996)
XLA Ops:
  0.6 88.5 %clip_conv.1 = (bf16[4,128,512]{2,1,0:T(8,128)(2,1)}, bf16[8,128,512]{2,1,0:T(8,128)(2,1)}, bf16[8,2,3,16,128]{4,3,2,1,0:T(8,128)(2,1)}) custom-call(s32[1,8]{1,0:T(1,128)} %lengths.1, bf16[8,128,512]{2,1,0:T(8,128)(2,1)} %bitcast.8, bf16[3,32,512]{2,1,0:T(8,128)(2,1)} %wt_own.1, bf16[3,32,512]{2,1,0:T(8,128)(2,1)} %wd_own.1, bf16[4,128,512]{2,1,0:T(8,128)(2,1)} %bitcast.11), custom_call_target="tpu_custom_call" | custom-call | tf_op jit(solution)/shard_map/clip_conv/pallas_call | solution.py:534
  89.1 1.0 %convert_bitcast_fusion = f32[2,3,2,16,4,128]{5,3,1,2,4,0:T(8,128)S(1)} fusion(bf16[2,4,2,3,16,128]{5,4,3,2,1,0:T(8,128)(2,1)} %bitcast.12), kind=kLoop, calls=%fused_computation | loop fusion | flops 98304 | bytes 589824 | tf_op jit(solution)/shard_map/convert_element_type | solution.py:590
  90.1 0.0 copy-start.1
  90.1 0.1 copy.10
  90.3 0.0 copy-start
  90.3 0.8 squeeze.15
  91.0 0.1 copy.9
  91.2 0.8 squeeze.14
  91.9 0.0 copy-done.1
  91.9 0.8 copy.13
  92.7 0.0 copy-done
  92.7 1.0 %copy.14 = bf16[1,8,128,512]{3,2,1,0:T(8,128)(2,1)} copy(bf16[1,8,128,512]{3,2,1,0:T(8,128)(2,1)S(1)} %bitcast.9) | data formatting | bytes 2097152
  (1 shorter events, 0.0 us)
Async XLA Ops:
  90.1 1.8 %copy-start.1 = (bf16[4,128,512]{2,1,0:T(8,128)(2,1)S(1)}, bf16[4,128,512]{2,1,0:T(8,128)(2,1)}, u32[]{:S(2)}) copy-start(bf16[4,128,512]{2,1,0:T(8,128)(2,1)} %get-tuple-element.7) | copy-start | bytes 1572868
  90.3 2.5 %copy-start = (bf16[8,128,512]{2,1,0:T(8,128)(2,1)S(1)}, bf16[8,128,512]{2,1,0:T(8,128)(2,1)}, u32[]{:S(2)}) copy-start(bf16[8,128,512]{2,1,0:T(8,128)(2,1)} %get-tuple-element.8) | copy-start | bytes 3145732

commit v2 on v1

v2 whole, which is shorter than its diff:
```python
import functools

import jax
import jax.numpy as jnp
from jax import lax
from jax.experimental import pallas as pl
from jax.experimental.pallas import tpu as pltpu
from jax.sharding import PartitionSpec as P

MESH = pl.DeviceIdType.MESH
BF = jnp.bfloat16
F32 = jnp.float32
FD, HD, S, C, NC = 8, 4, 128, 512, 8
NT = 16
NZ = 8
EPS = 1e-06


def dot(a, b, ca, cb):
    return lax.dot_general(a, b, (((ca,), (cb,)), ((), ())), preferred_element_type=F32)


def device(x, y, z, core):
    return {"tm": y * 4 + (x // 2) * 2 + core, "group": z * 2 + x % 2}


def kernel(
    lengths,
    clips_in,
    wt_own,
    wd_own,
    cot_in,
    reduced_out,
    clips_out,
    pieces,
    clips,
    reduced,
    grad_clips,
    wt,
    wd,
    clips_halo,
    cot_ext,
    h_ext,
    taps,
    gh,
    gm,
    hid,
    dtaps,
    gtap,
    stage,
    acc,
    core_out,
    core_in,
    outer_out,
    outer_in,
    inner_out,
    inner_in,
    z_wide,
    z_out,
    z_in,
    piece,
    w_send,
    w_recv,
    halo_send,
    halo_recv,
    core_send,
    core_recv,
    outer_send,
    outer_recv,
    inner_send,
    inner_recv,
    z_send,
    z_recv,
    p_send,
    p_recv,
    l_sem,
):
    t = lax.axis_index("tm")
    group = lax.axis_index("group")
    y, xh, c = t // 4, (t // 2) % 2, t % 2
    z, xl = group // 2, group % 2
    x = 2 * xh + xl

    def at(dx, dy, dz, dc):
        return device((x + dx + 4) % 4, (y + dy + 4) % 4, (z + dz + NZ) % NZ, (c + dc) % 2)

    sibling = at(0, 0, 0, 1)
    up, down = at(0, 1, 0, 0), at(0, -1, 0, 0)
    mirror = device(3 - x, y, z, c)
    step = 2 * c - 1
    far = {"tm": (t + step + NT) % NT, "group": group}

    def remote(src, dst, send, recv, target):
        return pltpu.make_async_remote_copy(
            src_ref=src,
            dst_ref=dst,
            send_sem=send,
            recv_sem=recv,
            device_id=target,
            device_id_type=MESH,
        )

    barrier = pltpu.get_barrier_semaphore()
    peers = [sibling, far]
    peers += [at(d, 0, 0, 0) for d in range(1, 4)] + [at(0, d, 0, 0) for d in range(1, 4)]
    peers += [at(0, 0, d, 0) for d in range(1, NZ)]
    mate = 1 - 2 * xl
    peers += [at(mate, 0, d, 0) for d in range(1, NZ)]
    for peer in peers:
        pl.semaphore_signal(barrier, inc=1, device_id=peer, device_id_type=MESH)
    pl.semaphore_wait(barrier, len(peers))

    def clips_copy(target):
        return remote(
            clips_in.at[pl.ds(FD - 4, 4)], clips_halo, halo_send.at[0], halo_recv.at[0], target
        )

    def cot_copy(target):
        return remote(
            cot_in.at[pl.ds(0, 2)], cot_ext.at[pl.ds(HD, 2)], halo_send.at[1], halo_recv.at[1], target
        )

    after = {"tm": (t + 1) % NT, "group": group}
    before = {"tm": (t + NT - 1) % NT, "group": group}

    mine = z % 2

    def cut(full, owner, half, lane, width):
        row = pl.multiple_of(owner * 32 + half * 16, 16)
        return full.at[:, pl.ds(row, 16), pl.ds(lane, width)]

    def owner_of(dy, other):
        h = 1 - xh if other else xh
        return ((y + dy + 4) % 4) * 4 + h * 2 + c

    blocks = [(0, 1), (-1, 0), (1, 0), (2, 0), (-1, 1), (1, 1), (2, 1)]
    ahead, behind = at(0, 0, 1, 0), at(0, 0, -1, 0)
    up2 = at(0, 2, 0, 0)

    def block_copy(w, number, slot, src, dst, to):
        return remote(src, dst, w_send.at[w, number], w_recv.at[w, slot], to)

    def half_copy(w, number, slot, owner, half, to, src=None):
        dst = cut((wd, wt)[w], owner, half, 0, C)
        return block_copy(w, number, slot, dst if src is None else src, dst, to)

    def lane_copy(w, number, slot, owner, half, lane, to):
        dst = cut((wd, wt)[w], owner, half, lane, C // 2)
        return block_copy(w, number, slot, dst, dst, to)

    def whole(w, owner):
        return (wd, wt)[w].at[:, pl.ds(pl.multiple_of(owner * 32, 32), 32), :]

    def first_sends(w):
        own = (wd_own, wt_own)[w]
        half = own.at[:, pl.ds(pl.multiple_of(mine * 16, 16), 16), :]
        return [
            half_copy(w, 0, 0, t, mine, mirror, half),
            half_copy(w, 1, 1, t, mine, up, half),
            half_copy(w, 2, 2, t, mine, down, half),
            half_copy(w, 3, 3, t, mine, up2, half),
            block_copy(w, 4, 21, own, whole(w, t), sibling),
        ]

    def passes(w, index):
        owner = owner_of(*blocks[index])
        sends = []
        if index == 0:
            sends = [
                half_copy(w, 5, 4, owner, mine, up),
                half_copy(w, 6, 5, owner, mine, down),
                half_copy(w, 7, 6, owner, mine, up2),
            ]
        return sends + [
            lane_copy(w, 8 + index, 7 + index, owner, mine, 0, ahead),
            lane_copy(w, 15 + index, 14 + index, owner, mine, C // 2, behind),
            half_copy(w, 22 + index, 22 + index, owner, mine, sibling),
        ]

    def last_pass(w, index):
        owner = owner_of(*blocks[index])
        return half_copy(w, 29 + index, 29 + index, owner, 1 - mine, sibling)

    def own_copy(w):
        return pltpu.make_async_copy((wd_own, wt_own)[w], whole(w, t), l_sem.at[w])

    def arrive(w, *indices):
        for index in indices:
            owner = owner_of(*blocks[index])
            half_copy(w, 0, index, owner, mine, sibling).wait_recv()
            for copy in passes(w, index):
                copy.start()

    def arrive_z(w, *indices):
        for index in indices:
            owner = owner_of(*blocks[index])
            lane_copy(w, 0, 7 + index, owner, 1 - mine, 0, sibling).wait_recv()
            lane_copy(w, 0, 14 + index, owner, 1 - mine, C // 2, sibling).wait_recv()
            last_pass(w, index).start()

    def finish_weights(w):
        own_copy(w).wait()
        other = 1 - 2 * c
        block_copy(w, 0, 21, whole(w, t + other), whole(w, t + other), sibling).wait_recv()
        for index in range(7):
            owner = owner_of(*blocks[index]) + other
            half_copy(w, 0, 22 + index, owner, mine, sibling).wait_recv()
            half_copy(w, 0, 29 + index, owner, 1 - mine, sibling).wait_recv()

    clips_load = pltpu.make_async_copy(clips_in, clips, l_sem.at[2])
    cot_load = pltpu.make_async_copy(cot_in, cot_ext.at[pl.ds(0, HD)], l_sem.at[3])
    clips_load.start()
    cot_load.start()

    @pl.when(t > 0)
    def _():
        cot_copy(before).start()

    for copy in first_sends(0):
        copy.start()

    @pl.when(t < NT - 1)
    def _():
        clips_copy(after).start()

    for copy in first_sends(1):
        copy.start()
    own_copy(0).start()
    own_copy(1).start()

    def length(i):
        return lengths[0, i]

    ends = [length(0)]
    for i in range(1, NC):
        ends.append(ends[-1] + length(i))
    first = t * FD

    def opens(frame):
        f = first + frame
        hit = f == 0
        for end in ends:
            hit = jnp.logical_or(hit, f == end)
        return hit

    opening = {i: opens(i) for i in range(-3, 11)}

    def live(k, frame):
        if k == 0:
            return None
        out = jnp.logical_not(opening[frame])
        if k == 2:
            out = jnp.logical_and(out, jnp.logical_not(opening[frame - 1]))
        return out

    def masked(keep, value):
        return value if keep is None else jnp.where(keep, value, jnp.zeros_like(value))

    def features(block):
        wide = block.astype(F32)
        scale = lax.rsqrt(jnp.mean(wide * wide, axis=-1, keepdims=True) + EPS)
        v = wide * scale
        return (v / (1.0 + jnp.exp(-v))).astype(BF)

    def feature_body(i, _):
        h_ext[4 + i] = features(clips[i])
        return 0

    clips_load.wait()
    lax.fori_loop(0, 4, feature_body, 0)
    arrive(0, 0, 1, 2)
    lax.fori_loop(4, FD, feature_body, 0)
    arrive(0, 3)
    arrive_z(0, 0, 1, 2)
    arrive(0, 4, 5)
    arrive_z(0, 3)
    arrive(0, 6)
    arrive(1, 0)
    arrive_z(0, 4, 5, 6)
    cot_load.wait()

    @pl.when(t < NT - 1)
    def _():
        cot_copy(before).wait_recv()

    @pl.when(t == NT - 1)
    def _():
        cot_ext[pl.ds(HD, 2)] = jnp.zeros((2, S, C), BF)

    finish_weights(0)

    flat0 = cot_ext[pl.ds(0, 5)].reshape(5 * S, C)
    flat1 = cot_ext[pl.ds(1, 5)].reshape(5 * S, C)
    p0 = dot(flat0, wd[0], 1, 1).reshape(5, S, C)
    for j in range(5):
        gh[2 * j] = p0[j]
    p2 = dot(flat1, wd[2], 1, 1).reshape(5, S, C)
    for j in range(5):
        total = gh[2 * j] + masked(live(2, 2 * j + 2), p2[j])
        gh[2 * j] = total
        gm[2 * j] = total.astype(BF)
    p1 = dot(flat1, wd[1], 1, 1).reshape(5, S, C)
    for j in range(5):
        total = masked(live(1, 2 * j + 2), p1[j])
        gh[2 * j + 1] = total
        gm[2 * j + 1] = total.astype(BF)

    arrive(1, 1, 2, 3)
    arrive_z(1, 0, 1, 2)

    @pl.when(t > 0)
    def _():
        clips_copy(after).wait_recv()

    @pl.when(t == 0)
    def _():
        clips_halo[...] = jnp.zeros((4, S, C), BF)

    def halo_body(i, _):
        h_ext[i] = features(clips_halo[i])
        return 0

    lax.fori_loop(0, 4, halo_body, 0)
    for k in range(3):
        for i in range(10):
            taps[k, i] = masked(live(k, i - 2), h_ext[i + 2 - k])

    def core_copy(g, k):
        return remote(
            core_out.at[g, k], core_in.at[g, k], core_send.at[g, k], core_recv.at[g, k], sibling
        )

    def contribute(g, k, value):
        stage[g] = value.reshape(4, 2, 2, 2, 16, C)
        for yy in range(4):
            for h in range(2):
                for l in range(2):
                    acc[g, k, 2 * h + l, yy] = stage[g, yy, h, c, l]
                    core_out[g, k, 2 * h + l, yy] = stage[g, yy, h, 1 - c, l].astype(BF)
        core_copy(g, k).start()

    def merge(g):
        for k in range(3):
            core_copy(g, k).wait_recv()
            acc[g, k] = acc[g, k] + core_in[g, k].astype(F32)

    def lanes(h):
        return pl.ds(h * (C // 2), C // 2)

    def line(h, d):
        return at(d, 0, 0, 0) if h == 0 else at(0, d, 0, 0)

    def outer_copy(g, h, d):
        i = 3 * h + d - 1
        return remote(
            outer_out.at[g, i],
            outer_in.at[g, i],
            outer_send.at[g, i],
            outer_recv.at[g, i],
            line(h, d),
        )

    def inner_copy(g, h, d):
        i = 3 * h + d - 1
        return remote(
            inner_out.at[g, i],
            inner_in.at[g, i],
            inner_send.at[g, i],
            inner_recv.at[g, i],
            line(1 - h, d),
        )

    order = [(h, d) for d in (2, 1, 3) for h in range(2)]

    def outer_start(g):
        for h, d in order:
            if h == 0:
                block = acc[g, :, (x + d) % 4, :, :, lanes(h)]
            else:
                block = acc[g, :, :, (y + d) % 4, :, lanes(h)]
            outer_out[g, 3 * h + d - 1] = block.astype(BF)
            outer_copy(g, h, d).start()

    def inner_start(g):
        for h, d in order:
            outer_copy(g, h, d).wait_recv()
        for h in range(2):
            ref = acc.at[g, :, x] if h == 0 else acc.at[g, :, :, y]
            total = ref[:, :, :, lanes(h)]
            for d in range(1, 4):
                total = total + outer_in[g, 3 * h + d - 1].astype(F32)
            ref[:, :, :, lanes(h)] = total
        for h, d in order:
            if h == 0:
                block = acc[g, :, x, (y + d) % 4, :, lanes(h)]
            else:
                block = acc[g, :, (x + d) % 4, y, :, lanes(h)]
            inner_out[g, 3 * h + d - 1] = block.astype(BF)
            inner_copy(g, h, d).start()

    def z_copy(g, d):
        return remote(
            z_out.at[g, (z + d) % NZ],
            z_in.at[g, d - 1],
            z_send.at[g, d - 1],
            z_recv.at[g, d - 1],
            at(0, 0, d, 0),
        )

    def z_start(g):
        for h, d in order:
            inner_copy(g, h, d).wait_recv()
        for h in range(2):
            total = acc[g, :, x, y, :, lanes(h)]
            for d in range(1, 4):
                total = total + inner_in[g, 3 * h + d - 1].astype(F32)
            for r in range(2):
                for q in range(2):
                    part = total[:, r * 8 : r * 8 + 8, q * 128 : q * 128 + 128]
                    z_wide[g, r * 4 + h * 2 + q] = part
                    z_out[g, r * 4 + h * 2 + q] = part.astype(BF)
        for d in (4, 3, 5, 2, 6, 1, 7):
            z_copy(g, d).start()

    def piece_copy(g, other, d):
        number = other * NZ + d - 1
        return remote(
            piece.at[g],
            pieces.at[g, z, xl],
            p_send.at[g, number],
            p_recv.at[g, number],
            at(mate * other, 0, d, 0),
        )

    sends = [(other, d) for d in (4, 3, 5, 2, 6, 1, 7) for other in (1, 0)] + [(1, 0)]

    def piece_start(g):
        total = z_wide[g, z]
        for d in range(1, NZ):
            z_copy(g, d).wait_recv()
            total = total + z_in[g, d - 1].astype(F32)
        piece[g] = total.astype(BF)
        for other, d in sends:
            piece_copy(g, other, d).start()
        pieces[g, z, xl] = piece[g]

    def time_grad(k):
        left = taps[k, pl.ds(2, FD)].reshape(FD * S, C)
        contribute(0, k, dot(left, gm[pl.ds(0, FD)].reshape(FD * S, C), 0, 0))

    time_grad(0)
    arrive(1, 4, 5)
    arrive_z(1, 3)
    time_grad(1)
    arrive(1, 6)
    time_grad(2)
    arrive_z(1, 4, 5, 6)
    for k in range(1, 3):
        for f in range(FD):
            gtap[k - 1, f] = masked(live(k, f + k), gm[f + k])
    merge(0)
    outer_start(0)
    finish_weights(1)

    def hidden_pair(i, wide):
        total = wide
        for k in range(3):
            total = total + dot(taps[k, pl.ds(i, 2)].reshape(2 * S, C), wt[k], 1, 0)
        hid[pl.ds(i, 2)] = total.astype(BF).reshape(2, S, C)

    hidden_pair(0, clips_halo[pl.ds(2, 2)].astype(F32).reshape(2 * S, C))

    def hidden_body(i, _):
        hidden_pair(2 + 2 * i, clips[pl.ds(2 * i, 2)].astype(F32).reshape(2 * S, C))
        return 0

    lax.fori_loop(0, FD // 2, hidden_body, 0)
    for k in range(3):
        for j in range(HD):
            dtaps[k, j] = masked(live(k, 2 * j), hid[2 * j + 2 - k])

    def down_grad(k):
        contribute(1, k, dot(dtaps[k].reshape(HD * S, C), cot_ext[pl.ds(0, HD)].reshape(HD * S, C), 0, 0))

    down_grad(0)
    down_grad(1)
    down_grad(2)
    total = dot(dtaps[0].reshape(HD * S, C), wd[0], 1, 0)
    total = total + dot(dtaps[1].reshape(HD * S, C), wd[1], 1, 0)
    total = total + dot(dtaps[2].reshape(HD * S, C), wd[2], 1, 0)
    reduced[...] = total.astype(BF).reshape(HD, S, C)
    reduced_store = pltpu.make_async_copy(reduced, reduced_out, l_sem.at[4])
    reduced_store.start()
    merge(1)
    outer_start(1)
    inner_start(0)

    def clips_pair(i, _):
        here = pl.ds(2 * i, 2)
        g = dot(gm[here].reshape(2 * S, C), wt[0], 1, 1)
        g = g + dot(gtap[0, here].reshape(2 * S, C), wt[1], 1, 1)
        g = g + dot(gtap[1, here].reshape(2 * S, C), wt[2], 1, 1)
        wide = clips[here].astype(F32).reshape(2 * S, C)
        scale = lax.rsqrt(jnp.mean(wide * wide, axis=-1, keepdims=True) + EPS)
        v = wide * scale
        sig = 1.0 / (1.0 + jnp.exp(-v))
        d = g * (sig * (1.0 + v * (1.0 - sig)))
        inner = jnp.mean(d * v, axis=-1, keepdims=True)
        grad = (d - v * inner) * scale
        grad_clips[here] = (gh[here].reshape(2 * S, C) + grad).astype(BF).reshape(2, S, C)
        return 0

    lax.fori_loop(0, 2, clips_pair, 0)
    z_start(0)
    lax.fori_loop(2, 3, clips_pair, 0)
    inner_start(1)
    lax.fori_loop(3, 4, clips_pair, 0)
    clips_store = pltpu.make_async_copy(grad_clips, clips_out, l_sem.at[5])
    clips_store.start()
    piece_start(0)
    z_start(1)
    piece_start(1)
    for g in range(2):
        for other, d in sends:
            piece_copy(g, other, d).wait()
    reduced_store.wait()
    clips_store.wait()

    @pl.when(t > 0)
    def _():
        cot_copy(before).wait_send()

    @pl.when(t < NT - 1)
    def _():
        clips_copy(after).wait_send()

    for w in range(2):
        for copy in first_sends(w):
            copy.wait_send()
        for index in range(7):
            for copy in passes(w, index):
                copy.wait_send()
            last_pass(w, index).wait_send()
    for g in range(2):
        for k in range(3):
            core_copy(g, k).wait_send()
        for h, d in order:
            outer_copy(g, h, d).wait_send()
            inner_copy(g, h, d).wait_send()
        for d in range(1, NZ):
            z_copy(g, d).wait_send()


def shards(clips, lengths, w_time, w_down, cotangent):
    vmem = pl.BlockSpec(memory_space=pltpu.VMEM)
    hbm = pl.BlockSpec(memory_space=pl.ANY)
    dma = pltpu.SemaphoreType.DMA
    reduced, grad_clips, pieces = pl.pallas_call(
        kernel,
        out_shape=(
            jax.ShapeDtypeStruct((HD, S, C), BF),
            jax.ShapeDtypeStruct((FD, S, C), BF),
            jax.ShapeDtypeStruct((2, NZ, 2, 3, 8, 128), BF),
        ),
        in_specs=[pl.BlockSpec(memory_space=pltpu.SMEM)] + [hbm] * 4,
        out_specs=(hbm, hbm, vmem),
        scratch_shapes=[
            pltpu.VMEM((FD, S, C), BF),
            pltpu.VMEM((HD, S, C), BF),
            pltpu.VMEM((FD, S, C), BF),
            pltpu.VMEM((3, C, C), BF),
            pltpu.VMEM((3, C, C), BF),
            pltpu.VMEM((4, S, C), BF),
            pltpu.VMEM((HD + 2, S, C), BF),
            pltpu.VMEM((FD + 4, S, C), BF),
            pltpu.VMEM((3, FD + 2, S, C), BF),
            pltpu.VMEM((FD + 2, S, C), F32),
            pltpu.VMEM((FD + 2, S, C), BF),
            pltpu.VMEM((FD + 2, S, C), BF),
            pltpu.VMEM((3, HD, S, C), BF),
            pltpu.VMEM((2, FD, S, C), BF),
            pltpu.VMEM((2, 4, 2, 2, 2, 16, C), F32),
            pltpu.VMEM((2, 3, 4, 4, 16, C), F32),
            pltpu.VMEM((2, 3, 4, 4, 16, C), BF),
            pltpu.VMEM((2, 3, 4, 4, 16, C), BF),
            pltpu.VMEM((2, 6, 3, 4, 16, C // 2), BF),
            pltpu.VMEM((2, 6, 3, 4, 16, C // 2), BF),
            pltpu.VMEM((2, 6, 3, 16, C // 2), BF),
            pltpu.VMEM((2, 6, 3, 16, C // 2), BF),
            pltpu.VMEM((2, NZ, 3, 8, 128), F32),
            pltpu.VMEM((2, NZ, 3, 8, 128), BF),
            pltpu.VMEM((2, NZ - 1, 3, 8, 128), BF),
            pltpu.VMEM((2, 3, 8, 128), BF),
            dma((2, 36)),
            dma((2, 36)),
            dma((2,)),
            dma((2,)),
            dma((2, 3)),
            dma((2, 3)),
            dma((2, 6)),
            dma((2, 6)),
            dma((2, 6)),
            dma((2, 6)),
            dma((2, NZ - 1)),
            dma((2, NZ - 1)),
            dma((2, 2 * NZ)),
            dma((2, 2 * NZ)),
            dma((6,)),
        ],
        name="clip_conv",
        compiler_params=pltpu.CompilerParams(
            collective_id=0, has_side_effects=True, vmem_limit_bytes=60 * 2**20
        ),
    )(lengths, clips[0], w_time, w_down, cotangent[0])
    grads = pieces.reshape(2, 2, 4, 2, 3, 8, 128).transpose(0, 4, 3, 1, 5, 2, 6)
    grads = grads.reshape(2, 3, 32, C).astype(F32)
    return reduced[None], grad_clips[None], grads[0], grads[1]


def solution(mesh):
    in_specs = (
        P("group", "tm", None, None),
        P("group", None),
        P(None, "tm", None),
        P(None, "tm", None),
        P("group", "tm", None, None),
    )
    out_specs = (
        P("group", "tm", None, None),
        P("group", "tm", None, None),
        P(None, "tm", None),
        P(None, "tm", None),
    )
    return jax.shard_map(shards, mesh=mesh, in_specs=in_specs, out_specs=out_specs, check_vma=False)
```

time: 93.8 us -> 80 us (0.85)
  Pallas kernels: 88.5 us -> 75 us
    pallas_call x1, Pallas kernels: 88.5 us -> 75 us  [shards(): pl.pallas_call(kernel, out_shape=(jax.ShapeDtypeStruct((HD, S, C), BF), j...]
    squeeze x2 -> x0, local copies, waits for them, and re-layouts: 1.51 us -> none  [shards(): return (reduced[None], grad_clips[None], grads[0], grads[1])]
    slice x3, local copies, waits for them, and re-layouts: 0.29 us -> 1.42 us  [shards(): return (reduced[None], grad_clips[None], grads[0], grads[1])]
where the time goes in v2:
time: 80 us; the launch traced here: 79.8 us
  Pallas kernels  75 us (94%)
  local copies, waits for them, and re-layouts  3.19 us (4%)
  other arithmetic  0.96 us (1%)
    pallas_call x1, Pallas kernels, shards(): pl.pallas_call(kernel, out_shape=(jax.ShapeDtypeStruct((HD, S, C), BF), j...  75 us
    unnamed x6, local copies, waits for them, and re-layouts  1.77 us

profile of v2, /device:TPU:2, one launch (start us, length us, event | category | flops | bytes accessed | tf_op | source)
XLA Modules:
  0.0 79.8 jit_solution(2192388451343628498)
XLA Ops:
  0.6 75.0 %clip_conv.1 = (bf16[4,128,512]{2,1,0:T(8,128)(2,1)}, bf16[8,128,512]{2,1,0:T(8,128)(2,1)}, bf16[2,8,2,3,8,128]{5,4,3,2,1,0:T(8,128)(2,1)}) custom-call(s32[1,8]{1,0:T(1,128)} %lengths.1, bf16[8,128,512]{2,1,0:T(8,128)(2,1)} %bitcast.10, bf16[3,32,512]{2,1,0:T(8,128)(2,1)} %wt_own.1, bf16[3,32,512]{2,1,0:T(8,128)(2,1)} %wd_own.1, bf16[4,128,512]{2,1,0:T(8,128)(2,1)} %bitcast.13), custom_call_target="tpu_custom_call" | custom-call | tf_op jit(solution)/shard_map/clip_conv/pallas_call | solution.py:558
  75.7 1.0 %convert_bitcast_fusion = f32[2,3,2,2,8,4,128]{6,4,1,2,5,3,0:T(8,128)S(1)} fusion(bf16[2,2,4,2,3,8,128]{6,5,4,3,2,1,0:T(8,128)(2,1)} %bitcast.16), kind=kLoop, calls=%fused_computation | loop fusion | flops 98304 | bytes 589824 | tf_op jit(solution)/shard_map/convert_element_type | solution.py:616
  76.6 0.0 copy-start.1
  76.7 0.0 copy-start
  76.7 0.7 copy.10
  77.4 0.7 copy.9
  78.1 0.0 copy-done.1
  78.1 0.8 copy.13
  78.9 0.0 copy-done
  78.9 1.0 %copy.14 = bf16[1,8,128,512]{3,2,1,0:T(8,128)(2,1)} copy(bf16[1,8,128,512]{3,2,1,0:T(8,128)(2,1)S(1)} %bitcast.11) | data formatting | bytes 2097152
  (1 shorter events, 0.0 us)
Async XLA Ops:
  76.6 1.4 %copy-start.1 = (bf16[4,128,512]{2,1,0:T(8,128)(2,1)S(1)}, bf16[4,128,512]{2,1,0:T(8,128)(2,1)}, u32[]{:S(2)}) copy-start(bf16[4,128,512]{2,1,0:T(8,128)(2,1)} %get-tuple-element.7) | copy-start | bytes 1572868
  76.7 2.2 %copy-start = (bf16[8,128,512]{2,1,0:T(8,128)(2,1)S(1)}, bf16[8,128,512]{2,1,0:T(8,128)(2,1)}, u32[]{:S(2)}) copy-start(bf16[8,128,512]{2,1,0:T(8,128)(2,1)} %get-tuple-element.8) | copy-start | bytes 3145732

commit v3 on v2

--- a/solution.py
+++ b/solution.py
@@ -223,8 +223,6 @@
     def _():
         clips_copy(after).start()
 
-    for copy in first_sends(1):
-        copy.start()
     own_copy(0).start()
     own_copy(1).start()
 
@@ -267,16 +265,18 @@
         return 0
 
     clips_load.wait()
-    lax.fori_loop(0, 4, feature_body, 0)
-    arrive(0, 0, 1, 2)
-    lax.fori_loop(4, FD, feature_body, 0)
-    arrive(0, 3)
-    arrive_z(0, 0, 1, 2)
-    arrive(0, 4, 5)
-    arrive_z(0, 3)
-    arrive(0, 6)
+    lax.fori_loop(0, 2, feature_body, 0)
+    arrive(0, 0)
+    for copy in first_sends(1):
+        copy.start()
+    lax.fori_loop(2, 4, feature_body, 0)
+    arrive(0, 1, 2, 3)
+    lax.fori_loop(4, 6, feature_body, 0)
     arrive(1, 0)
-    arrive_z(0, 4, 5, 6)
+    arrive(0, 4, 5, 6)
+    lax.fori_loop(6, FD, feature_body, 0)
+    arrive(1, 1, 2, 3)
+    arrive_z(0, 0, 1, 2, 3, 4, 5, 6)
     cot_load.wait()
 
     @pl.when(t < NT - 1)
@@ -294,6 +294,7 @@
     p0 = dot(flat0, wd[0], 1, 1).reshape(5, S, C)
     for j in range(5):
         gh[2 * j] = p0[j]
+    arrive(1, 4, 5, 6)
     p2 = dot(flat1, wd[2], 1, 1).reshape(5, S, C)
     for j in range(5):
         total = gh[2 * j] + masked(live(2, 2 * j + 2), p2[j])
@@ -305,8 +306,7 @@
         gh[2 * j + 1] = total
         gm[2 * j + 1] = total.astype(BF)
 
-    arrive(1, 1, 2, 3)
-    arrive_z(1, 0, 1, 2)
+    arrive_z(1, 0, 1, 2, 3)
 
     @pl.when(t > 0)
     def _():
@@ -339,24 +339,19 @@
                     core_out[g, k, 2 * h + l, yy] = stage[g, yy, h, 1 - c, l].astype(BF)
         core_copy(g, k).start()
 
-    def merge(g):
-        for k in range(3):
-            core_copy(g, k).wait_recv()
-            acc[g, k] = acc[g, k] + core_in[g, k].astype(F32)
-
     def lanes(h):
         return pl.ds(h * (C // 2), C // 2)
 
     def line(h, d):
         return at(d, 0, 0, 0) if h == 0 else at(0, d, 0, 0)
 
-    def outer_copy(g, h, d):
+    def outer_copy(g, k, h, d):
         i = 3 * h + d - 1
         return remote(
-            outer_out.at[g, i],
-            outer_in.at[g, i],
-            outer_send.at[g, i],
-            outer_recv.at[g, i],
+            outer_out.at[g, k, i],
+            outer_in.at[g, k, i],
+            outer_send.at[g, k, i],
+            outer_recv.at[g, k, i],
             line(h, d),
         )
 
@@ -372,24 +367,27 @@
 
     order = [(h, d) for d in (2, 1, 3) for h in range(2)]
 
-    def outer_start(g):
+    def reduce_tap(g, k):
+        core_copy(g, k).wait_recv()
+        acc[g, k] = acc[g, k] + core_in[g, k].astype(F32)
         for h, d in order:
             if h == 0:
-                block = acc[g, :, (x + d) % 4, :, :, lanes(h)]
+                block = acc[g, k, (x + d) % 4, :, :, lanes(h)]
             else:
-                block = acc[g, :, :, (y + d) % 4, :, lanes(h)]
-            outer_out[g, 3 * h + d - 1] = block.astype(BF)
-            outer_copy(g, h, d).start()
+                block = acc[g, k, :, (y + d) % 4, :, lanes(h)]
+            outer_out[g, k, 3 * h + d - 1] = block.astype(BF)
+            outer_copy(g, k, h, d).start()
 
     def inner_start(g):
-        for h, d in order:
-            outer_copy(g, h, d).wait_recv()
-        for h in range(2):
-            ref = acc.at[g, :, x] if h == 0 else acc.at[g, :, :, y]
-            total = ref[:, :, :, lanes(h)]
-            for d in range(1, 4):
-                total = total + outer_in[g, 3 * h + d - 1].astype(F32)
-            ref[:, :, :, lanes(h)] = total
+        for k in range(3):
+            for h, d in order:
+                outer_copy(g, k, h, d).wait_recv()
+            for h in range(2):
+                ref = acc.at[g, k, x] if h == 0 else acc.at[g, k, :, y]
+                total = ref[:, :, lanes(h)]
+                for d in range(1, 4):
+                    total = total + outer_in[g, k, 3 * h + d - 1].astype(F32)
+                ref[:, :, lanes(h)] = total
         for h, d in order:
             if h == 0:
                 block = acc[g, :, x, (y + d) % 4, :, lanes(h)]
@@ -449,17 +447,15 @@
         contribute(0, k, dot(left, gm[pl.ds(0, FD)].reshape(FD * S, C), 0, 0))
 
     time_grad(0)
-    arrive(1, 4, 5)
-    arrive_z(1, 3)
+    arrive_z(1, 4, 5, 6)
     time_grad(1)
-    arrive(1, 6)
+    reduce_tap(0, 0)
     time_grad(2)
-    arrive_z(1, 4, 5, 6)
+    reduce_tap(0, 1)
     for k in range(1, 3):
         for f in range(FD):
             gtap[k - 1, f] = masked(live(k, f + k), gm[f + k])
-    merge(0)
-    outer_start(0)
+    reduce_tap(0, 2)
     finish_weights(1)
 
     def hidden_pair(i, wide):
@@ -485,14 +481,15 @@
     down_grad(0)
     down_grad(1)
     down_grad(2)
+    reduce_tap(1, 0)
     total = dot(dtaps[0].reshape(HD * S, C), wd[0], 1, 0)
     total = total + dot(dtaps[1].reshape(HD * S, C), wd[1], 1, 0)
+    reduce_tap(1, 1)
     total = total + dot(dtaps[2].reshape(HD * S, C), wd[2], 1, 0)
     reduced[...] = total.astype(BF).reshape(HD, S, C)
     reduced_store = pltpu.make_async_copy(reduced, reduced_out, l_sem.at[4])
     reduced_store.start()
-    merge(1)
-    outer_start(1)
+    reduce_tap(1, 2)
     inner_start(0)
 
     def clips_pair(i, _):
@@ -545,7 +542,8 @@
         for k in range(3):
             core_copy(g, k).wait_send()
         for h, d in order:
-            outer_copy(g, h, d).wait_send()
+            for k in range(3):
+                outer_copy(g, k, h, d).wait_send()
             inner_copy(g, h, d).wait_send()
         for d in range(1, NZ):
             z_copy(g, d).wait_send()
@@ -583,8 +581,8 @@
             pltpu.VMEM((2, 3, 4, 4, 16, C), F32),
             pltpu.VMEM((2, 3, 4, 4, 16, C), BF),
             pltpu.VMEM((2, 3, 4, 4, 16, C), BF),
-            pltpu.VMEM((2, 6, 3, 4, 16, C // 2), BF),
-            pltpu.VMEM((2, 6, 3, 4, 16, C // 2), BF),
+            pltpu.VMEM((2, 3, 6, 4, 16, C // 2), BF),
+            pltpu.VMEM((2, 3, 6, 4, 16, C // 2), BF),
             pltpu.VMEM((2, 6, 3, 16, C // 2), BF),
             pltpu.VMEM((2, 6, 3, 16, C // 2), BF),
             pltpu.VMEM((2, NZ, 3, 8, 128), F32),
@@ -597,8 +595,8 @@
             dma((2,)),
             dma((2, 3)),
             dma((2, 3)),
-            dma((2, 6)),
-            dma((2, 6)),
+            dma((2, 3, 6)),
+            dma((2, 3, 6)),
             dma((2, 6)),
             dma((2, 6)),
             dma((2, NZ - 1)),
@@ -612,9 +610,53 @@
             collective_id=0, has_side_effects=True, vmem_limit_bytes=60 * 2**20
         ),
     )(lengths, clips[0], w_time, w_down, cotangent[0])
-    grads = pieces.reshape(2, 2, 4, 2, 3, 8, 128).transpose(0, 4, 3, 1, 5, 2, 6)
-    grads = grads.reshape(2, 3, 32, C).astype(F32)
-    return reduced[None], grad_clips[None], grads[0], grads[1]
+    reduced, grad_clips, grad_time, grad_down = pl.pallas_call(
+        deliver,
+        out_shape=(
+            jax.ShapeDtypeStruct((HD, S, C), BF),
+            jax.ShapeDtypeStruct((FD, S, C), BF),
+            jax.ShapeDtypeStruct((3, 32, C), F32),
+            jax.ShapeDtypeStruct((3, 32, C), F32),
+        ),
+        in_specs=[hbm, hbm, vmem],
+        out_specs=(hbm, hbm, vmem, vmem),
+        scratch_shapes=[
+            pltpu.VMEM((FD + HD, S, C), BF),
+            dma((6,)),
+            dma((6,)),
+        ],
+        name="deliver",
+        compiler_params=pltpu.CompilerParams(vmem_limit_bytes=60 * 2**20),
+    )(reduced, grad_clips, pieces)
+    return reduced[None], grad_clips[None], grad_time, grad_down
+
+
+def deliver(reduced, grad_clips, pieces, reduced_out, clips_out, time_out, down_out, held, load, store):
+    def ends(i):
+        if i < 4:
+            return grad_clips.at[pl.ds(2 * i, 2)], clips_out.at[pl.ds(2 * i, 2)]
+        return reduced.at[pl.ds(2 * i - 8, 2)], reduced_out.at[pl.ds(2 * i - 8, 2)]
+
+    loads = [
+        pltpu.make_async_copy(ends(i)[0], held.at[pl.ds(2 * i, 2)], load.at[i]) for i in range(6)
+    ]
+    stores = [
+        pltpu.make_async_copy(held.at[pl.ds(2 * i, 2)], ends(i)[1], store.at[i]) for i in range(6)
+    ]
+    for copy in loads:
+        copy.start()
+    for g, out in ((0, time_out), (1, down_out)):
+        for r in range(2):
+            for q in range(4):
+                for l in range(2):
+                    out[:, l * 16 + r * 8 : l * 16 + r * 8 + 8, q * 128 : q * 128 + 128] = pieces[
+                        g, r * 4 + q, l
+                    ].astype(F32)
+    for i in range(6):
+        loads[i].wait()
+        stores[i].start()
+    for copy in stores:
+        copy.wait()
 
 
 def solution(mesh):

time: 80 us -> 75.4 us (0.943)
  local copies, waits for them, and re-layouts: 3.19 us -> 0 us
  other arithmetic: 0.96 us -> 0 us
    pallas_call x1, Pallas kernels: 75 us -> 70.7 us  [shards(): pl.pallas_call(kernel, out_shape=(jax.ShapeDtypeStruct((HD, S, C), BF), j...]
    pallas_call x0 -> x1, Pallas kernels: none -> 3.86 us  [shards(): pl.pallas_call(deliver, out_shape=(jax.ShapeDtypeStruct((HD, S, C), BF),...]
    unnamed x6 -> x0, local copies, waits for them, and re-layouts: 1.77 us -> none
    slice x3 -> x0, local copies, waits for them, and re-layouts: 1.42 us -> none  [shards(): return (reduced[None], grad_clips[None], grads[0], grads[1])]
    convert_element_type x1 -> x0, other arithmetic: 0.96 us -> none  [shards(): grads = grads.reshape(2, 3, 32, C).astype(F32)]
where the time goes in v3:
time: 75.4 us; the launch traced here: 75.2 us
  Pallas kernels  74.6 us (99%)
    pallas_call x1, Pallas kernels, shards(): pl.pallas_call(kernel, out_shape=(jax.ShapeDtypeStruct((HD, S, C), BF), j...  70.7 us
    pallas_call x1, Pallas kernels, shards(): pl.pallas_call(deliver, out_shape=(jax.ShapeDtypeStruct((HD, S, C), BF),...  3.86 us

profile of v3, /device:TPU:2, one launch (start us, length us, event | category | flops | bytes accessed | tf_op | source)
XLA Modules:
  0.0 75.2 jit_solution(6053242563450557530)
XLA Ops:
  0.6 70.7 %clip_conv.1 = (bf16[4,128,512]{2,1,0:T(8,128)(2,1)}, bf16[8,128,512]{2,1,0:T(8,128)(2,1)}, bf16[2,8,2,3,8,128]{5,4,3,2,1,0:T(8,128)(2,1)}) custom-call(s32[1,8]{1,0:T(1,128)} %lengths.1, bf16[8,128,512]{2,1,0:T(8,128)(2,1)} %bitcast.4, bf16[3,32,512]{2,1,0:T(8,128)(2,1)} %wt_own.1, bf16[3,32,512]{2,1,0:T(8,128)(2,1)} %wd_own.1, bf16[4,128,512]{2,1,0:T(8,128)(2,1)} %bitcast.5), custom_call_target="tpu_custom_call" | custom-call | tf_op jit(solution)/shard_map/clip_conv/pallas_call | solution.py:556
  71.4 3.9 %deliver.1 = (bf16[4,128,512]{2,1,0:T(8,128)(2,1)}, bf16[8,128,512]{2,1,0:T(8,128)(2,1)}, f32[3,32,512]{2,1,0:T(8,128)}, f32[3,32,512]{2,1,0:T(8,128)}) custom-call(bf16[4,128,512]{2,1,0:T(8,128)(2,1)} %get-tuple-element.11.reduced, bf16[8,128,512]{2,1,0:T(8,128)(2,1)} %get-tuple-element.12.grad_clips, bf16[2,8,2,3,8,128]{5,4,3,2,1,0:T(8,128)(2,1)} %get-tuple-element.13.pieces), custom_call_target="tpu_custom_call" | custom-call | tf_op jit(solution)/shard_map/deliver/pallas_call | solution.py:613

commit v4 on v3

--- a/solution.py
+++ b/solution.py
@@ -25,17 +25,16 @@
 
 
 def kernel(
-    lengths,
+    lengths_in,
     clips_in,
     wt_own,
     wd_own,
     cot_in,
-    reduced_out,
-    clips_out,
-    pieces,
-    clips,
     reduced,
     grad_clips,
+    pieces,
+    lengths,
+    clips,
     wt,
     wd,
     clips_halo,
@@ -100,6 +99,9 @@
             device_id_type=MESH,
         )
 
+    lengths_load = pltpu.make_async_copy(lengths_in, lengths, l_sem.at[4])
+    lengths_load.start()
+
     barrier = pltpu.get_barrier_semaphore()
     peers = [sibling, far]
     peers += [at(d, 0, 0, 0) for d in range(1, 4)] + [at(0, d, 0, 0) for d in range(1, 4)]
@@ -110,14 +112,14 @@
         pl.semaphore_signal(barrier, inc=1, device_id=peer, device_id_type=MESH)
     pl.semaphore_wait(barrier, len(peers))
 
-    def clips_copy(target):
+    def clips_copy(f, target):
         return remote(
-            clips_in.at[pl.ds(FD - 4, 4)], clips_halo, halo_send.at[0], halo_recv.at[0], target
-        )
-
-    def cot_copy(target):
+            clips_in.at[FD - 4 + f], clips_halo.at[f], halo_send.at[f], halo_recv.at[f], target
+        )
+
+    def cot_copy(f, target):
         return remote(
-            cot_in.at[pl.ds(0, 2)], cot_ext.at[pl.ds(HD, 2)], halo_send.at[1], halo_recv.at[1], target
+            cot_in.at[f], cot_ext.at[HD + f], halo_send.at[4 + f], halo_recv.at[4 + f], target
         )
 
     after = {"tm": (t + 1) % NT, "group": group}
@@ -212,19 +214,23 @@
     clips_load.start()
     cot_load.start()
 
-    @pl.when(t > 0)
-    def _():
-        cot_copy(before).start()
+    def send_cot(f):
+        @pl.when(t > 0)
+        def _():
+            cot_copy(f, before).start()
+
+    def send_clips(f):
+        @pl.when(t < NT - 1)
+        def _():
+            clips_copy(f, after).start()
 
     for copy in first_sends(0):
         copy.start()
-
-    @pl.when(t < NT - 1)
-    def _():
-        clips_copy(after).start()
-
+    send_cot(0)
     own_copy(0).start()
     own_copy(1).start()
+
+    lengths_load.wait()
 
     def length(i):
         return lengths[0, i]
@@ -267,13 +273,18 @@
     clips_load.wait()
     lax.fori_loop(0, 2, feature_body, 0)
     arrive(0, 0)
+    send_cot(1)
     for copy in first_sends(1):
         copy.start()
+    send_clips(3)
     lax.fori_loop(2, 4, feature_body, 0)
     arrive(0, 1, 2, 3)
+    send_clips(2)
     lax.fori_loop(4, 6, feature_body, 0)
     arrive(1, 0)
+    send_clips(1)
     arrive(0, 4, 5, 6)
+    send_clips(0)
     lax.fori_loop(6, FD, feature_body, 0)
     arrive(1, 1, 2, 3)
     arrive_z(0, 0, 1, 2, 3, 4, 5, 6)
@@ -281,7 +292,8 @@
 
     @pl.when(t < NT - 1)
     def _():
-        cot_copy(before).wait_recv()
+        cot_copy(0, before).wait_recv()
+        cot_copy(1, before).wait_recv()
 
     @pl.when(t == NT - 1)
     def _():
@@ -310,7 +322,8 @@
 
     @pl.when(t > 0)
     def _():
-        clips_copy(after).wait_recv()
+        for f in range(4):
+            clips_copy(f, after).wait_recv()
 
     @pl.when(t == 0)
     def _():
@@ -487,8 +500,6 @@
     reduce_tap(1, 1)
     total = total + dot(dtaps[2].reshape(HD * S, C), wd[2], 1, 0)
     reduced[...] = total.astype(BF).reshape(HD, S, C)
-    reduced_store = pltpu.make_async_copy(reduced, reduced_out, l_sem.at[4])
-    reduced_store.start()
     reduce_tap(1, 2)
     inner_start(0)
 
@@ -512,24 +523,22 @@
     lax.fori_loop(2, 3, clips_pair, 0)
     inner_start(1)
     lax.fori_loop(3, 4, clips_pair, 0)
-    clips_store = pltpu.make_async_copy(grad_clips, clips_out, l_sem.at[5])
-    clips_store.start()
     piece_start(0)
     z_start(1)
     piece_start(1)
     for g in range(2):
         for other, d in sends:
             piece_copy(g, other, d).wait()
-    reduced_store.wait()
-    clips_store.wait()
 
     @pl.when(t > 0)
     def _():
-        cot_copy(before).wait_send()
+        cot_copy(0, before).wait_send()
+        cot_copy(1, before).wait_send()
 
     @pl.when(t < NT - 1)
     def _():
-        clips_copy(after).wait_send()
+        for f in range(4):
+            clips_copy(f, after).wait_send()
 
     for w in range(2):
         for copy in first_sends(w):
@@ -551,7 +560,8 @@
 
 def shards(clips, lengths, w_time, w_down, cotangent):
     vmem = pl.BlockSpec(memory_space=pltpu.VMEM)
-    hbm = pl.BlockSpec(memory_space=pl.ANY)
+    hbm = pl.BlockSpec(memory_space=pltpu.HBM)
+    pin = pltpu.with_memory_space_constraint
     dma = pltpu.SemaphoreType.DMA
     reduced, grad_clips, pieces = pl.pallas_call(
         kernel,
@@ -560,11 +570,10 @@
             jax.ShapeDtypeStruct((FD, S, C), BF),
             jax.ShapeDtypeStruct((2, NZ, 2, 3, 8, 128), BF),
         ),
-        in_specs=[pl.BlockSpec(memory_space=pltpu.SMEM)] + [hbm] * 4,
-        out_specs=(hbm, hbm, vmem),
+        in_specs=[hbm] * 5,
+        out_specs=(vmem, vmem, vmem),
         scratch_shapes=[
-            pltpu.VMEM((FD, S, C), BF),
-            pltpu.VMEM((HD, S, C), BF),
+            pltpu.SMEM((1, NC), jnp.int32),
             pltpu.VMEM((FD, S, C), BF),
             pltpu.VMEM((3, C, C), BF),
             pltpu.VMEM((3, C, C), BF),
@@ -591,8 +600,8 @@
             pltpu.VMEM((2, 3, 8, 128), BF),
             dma((2, 36)),
             dma((2, 36)),
-            dma((2,)),
-            dma((2,)),
+            dma((6,)),
+            dma((6,)),
             dma((2, 3)),
             dma((2, 3)),
             dma((2, 3, 6)),
@@ -603,13 +612,13 @@
             dma((2, NZ - 1)),
             dma((2, 2 * NZ)),
             dma((2, 2 * NZ)),
-            dma((6,)),
+            dma((5,)),
         ],
         name="clip_conv",
         compiler_params=pltpu.CompilerParams(
-            collective_id=0, has_side_effects=True, vmem_limit_bytes=60 * 2**20
+            collective_id=0, has_side_effects=True, vmem_limit_bytes=44 * 2**20
         ),
-    )(lengths, clips[0], w_time, w_down, cotangent[0])
+    )(*(pin(a, pltpu.HBM) for a in (lengths, clips[0], w_time, w_down, cotangent[0])))
     reduced, grad_clips, grad_time, grad_down = pl.pallas_call(
         deliver,
         out_shape=(
@@ -618,43 +627,32 @@
             jax.ShapeDtypeStruct((3, 32, C), F32),
             jax.ShapeDtypeStruct((3, 32, C), F32),
         ),
-        in_specs=[hbm, hbm, vmem],
-        out_specs=(hbm, hbm, vmem, vmem),
+        in_specs=[vmem] * 3,
+        out_specs=(hbm,) * 4,
         scratch_shapes=[
-            pltpu.VMEM((FD + HD, S, C), BF),
-            dma((6,)),
-            dma((6,)),
+            pltpu.VMEM((3, 32, C), F32),
+            pltpu.VMEM((3, 32, C), F32),
+            dma((4,)),
         ],
         name="deliver",
-        compiler_params=pltpu.CompilerParams(vmem_limit_bytes=60 * 2**20),
+        compiler_params=pltpu.CompilerParams(vmem_limit_bytes=16 * 2**20),
     )(reduced, grad_clips, pieces)
     return reduced[None], grad_clips[None], grad_time, grad_down
 
 
-def deliver(reduced, grad_clips, pieces, reduced_out, clips_out, time_out, down_out, held, load, store):
-    def ends(i):
-        if i < 4:
-            return grad_clips.at[pl.ds(2 * i, 2)], clips_out.at[pl.ds(2 * i, 2)]
-        return reduced.at[pl.ds(2 * i - 8, 2)], reduced_out.at[pl.ds(2 * i - 8, 2)]
-
-    loads = [
-        pltpu.make_async_copy(ends(i)[0], held.at[pl.ds(2 * i, 2)], load.at[i]) for i in range(6)
-    ]
-    stores = [
-        pltpu.make_async_copy(held.at[pl.ds(2 * i, 2)], ends(i)[1], store.at[i]) for i in range(6)
-    ]
-    for copy in loads:
-        copy.start()
-    for g, out in ((0, time_out), (1, down_out)):
+def deliver(reduced, grad_clips, pieces, reduced_out, clips_out, time_out, down_out, time, down, sem):
+    pairs = ((grad_clips, clips_out), (reduced, reduced_out), (time, time_out), (down, down_out))
+    stores = [pltpu.make_async_copy(a, b, sem.at[i]) for i, (a, b) in enumerate(pairs)]
+    stores[0].start()
+    stores[1].start()
+    for g, full in ((0, time), (1, down)):
         for r in range(2):
             for q in range(4):
                 for l in range(2):
-                    out[:, l * 16 + r * 8 : l * 16 + r * 8 + 8, q * 128 : q * 128 + 128] = pieces[
+                    full[:, l * 16 + r * 8 : l * 16 + r * 8 + 8, q * 128 : q * 128 + 128] = pieces[
                         g, r * 4 + q, l
                     ].astype(F32)
-    for i in range(6):
-        loads[i].wait()
-        stores[i].start()
+        stores[2 + g].start()
     for copy in stores:
         copy.wait()
 

time: 75.4 us -> 69.9 us (0.927)
  Pallas kernels: 74.6 us -> 69.1 us
    pallas_call x1, Pallas kernels: 70.7 us -> 67.8 us  [shards(): pl.pallas_call(kernel, out_shape=(jax.ShapeDtypeStruct((HD, S, C), BF), j...]
    pallas_call x1, Pallas kernels: 3.86 us -> 1.3 us  [shards(): pl.pallas_call(deliver, out_shape=(jax.ShapeDtypeStruct((HD, S, C), BF),...]
where the time goes in v4:
time: 69.9 us; the launch traced here: 69.8 us
  Pallas kernels  69.1 us (99%)
    pallas_call x1, Pallas kernels, shards(): pl.pallas_call(kernel, out_shape=(jax.ShapeDtypeStruct((HD, S, C), BF), j...  67.8 us

profile of v4, /device:TPU:2, one launch (start us, length us, event | category | flops | bytes accessed | tf_op | source)
XLA Modules:
  0.0 69.8 jit_solution(6086740641935450343)
XLA Ops:
  0.6 67.8 %clip_conv.1 = (bf16[4,128,512]{2,1,0:T(8,128)(2,1)S(1)}, bf16[8,128,512]{2,1,0:T(8,128)(2,1)S(1)}, bf16[2,8,2,3,8,128]{5,4,3,2,1,0:T(8,128)(2,1)S(1)}) custom-call(s32[1,8]{1,0:T(1,128)} %lengths_in.1, bf16[8,128,512]{2,1,0:T(8,128)(2,1)} %bitcast.4, bf16[3,32,512]{2,1,0:T(8,128)(2,1)} %wt_own.1, bf16[3,32,512]{2,1,0:T(8,128)(2,1)} %wd_own.1, ...), custom_call_target="tpu_custom_call" | custom-call | tf_op jit(solution)/shard_map/clip_conv/pallas_call | solution.py:566
  68.5 1.3 %deliver.1 = (bf16[4,128,512]{2,1,0:T(8,128)(2,1)}, bf16[8,128,512]{2,1,0:T(8,128)(2,1)}, f32[3,32,512]{2,1,0:T(8,128)}, f32[3,32,512]{2,1,0:T(8,128)}) custom-call(bf16[4,128,512]{2,1,0:T(8,128)(2,1)S(1)} %get-tuple-element.11.reduced, bf16[8,128,512]{2,1,0:T(8,128)(2,1)S(1)} %get-tuple-element.12.grad_clips, ...), custom_call_target="tpu_custom_call" | custom-call | tf_op jit(solution)/shard_map/deliver/pallas_call | solution.py:622

commit v5 on v4

--- a/solution.py
+++ b/solution.py
@@ -125,7 +125,7 @@
     after = {"tm": (t + 1) % NT, "group": group}
     before = {"tm": (t + NT - 1) % NT, "group": group}
 
-    mine = z % 2
+    mine = (z + xl) % 2
 
     def cut(full, owner, half, lane, width):
         row = pl.multiple_of(owner * 32 + half * 16, 16)
@@ -136,7 +136,7 @@
         return ((y + dy + 4) % 4) * 4 + h * 2 + c
 
     blocks = [(0, 1), (-1, 0), (1, 0), (2, 0), (-1, 1), (1, 1), (2, 1)]
-    ahead, behind = at(0, 0, 1, 0), at(0, 0, -1, 0)
+    ahead, behind, beside = at(0, 0, 1, 0), at(0, 0, -1, 0), at(mate, 0, 0, 0)
     up2 = at(0, 2, 0, 0)
 
     def block_copy(w, number, slot, src, dst, to):
@@ -146,8 +146,9 @@
         dst = cut((wd, wt)[w], owner, half, 0, C)
         return block_copy(w, number, slot, dst if src is None else src, dst, to)
 
-    def lane_copy(w, number, slot, owner, half, lane, to):
-        dst = cut((wd, wt)[w], owner, half, lane, C // 2)
+    def tap_copy(w, number, slot, owner, half, tap, to):
+        row = pl.multiple_of(owner * 32 + half * 16, 16)
+        dst = (wd, wt)[w].at[tap, pl.ds(row, 16), :]
         return block_copy(w, number, slot, dst, dst, to)
 
     def whole(w, owner):
@@ -156,8 +157,9 @@
     def first_sends(w):
         own = (wd_own, wt_own)[w]
         half = own.at[:, pl.ds(pl.multiple_of(mine * 16, 16), 16), :]
+        rest = own.at[:, pl.ds(pl.multiple_of(16 - mine * 16, 16), 16), :]
         return [
-            half_copy(w, 0, 0, t, mine, mirror, half),
+            half_copy(w, 0, 0, t, 1 - mine, mirror, rest),
             half_copy(w, 1, 1, t, mine, up, half),
             half_copy(w, 2, 2, t, mine, down, half),
             half_copy(w, 3, 3, t, mine, up2, half),
@@ -174,8 +176,9 @@
                 half_copy(w, 7, 6, owner, mine, up2),
             ]
         return sends + [
-            lane_copy(w, 8 + index, 7 + index, owner, mine, 0, ahead),
-            lane_copy(w, 15 + index, 14 + index, owner, mine, C // 2, behind),
+            tap_copy(w, 8 + index, 7 + index, owner, mine, 0, ahead),
+            tap_copy(w, 15 + index, 14 + index, owner, mine, 2, behind),
+            tap_copy(w, 36 + index, 36 + index, owner, mine, 1, beside),
             half_copy(w, 22 + index, 22 + index, owner, mine, sibling),
         ]
 
@@ -196,8 +199,9 @@
     def arrive_z(w, *indices):
         for index in indices:
             owner = owner_of(*blocks[index])
-            lane_copy(w, 0, 7 + index, owner, 1 - mine, 0, sibling).wait_recv()
-            lane_copy(w, 0, 14 + index, owner, 1 - mine, C // 2, sibling).wait_recv()
+            tap_copy(w, 0, 7 + index, owner, 1 - mine, 0, sibling).wait_recv()
+            tap_copy(w, 0, 14 + index, owner, 1 - mine, 2, sibling).wait_recv()
+            tap_copy(w, 0, 36 + index, owner, 1 - mine, 1, sibling).wait_recv()
             last_pass(w, index).start()
 
     def finish_weights(w):
@@ -276,17 +280,17 @@
     send_cot(1)
     for copy in first_sends(1):
         copy.start()
-    send_clips(3)
     lax.fori_loop(2, 4, feature_body, 0)
     arrive(0, 1, 2, 3)
-    send_clips(2)
+    send_clips(3)
     lax.fori_loop(4, 6, feature_body, 0)
     arrive(1, 0)
-    send_clips(1)
     arrive(0, 4, 5, 6)
-    send_clips(0)
+    send_clips(2)
     lax.fori_loop(6, FD, feature_body, 0)
     arrive(1, 1, 2, 3)
+    send_clips(1)
+    send_clips(0)
     arrive_z(0, 0, 1, 2, 3, 4, 5, 6)
     cot_load.wait()
 
@@ -320,24 +324,6 @@
 
     arrive_z(1, 0, 1, 2, 3)
 
-    @pl.when(t > 0)
-    def _():
-        for f in range(4):
-            clips_copy(f, after).wait_recv()
-
-    @pl.when(t == 0)
-    def _():
-        clips_halo[...] = jnp.zeros((4, S, C), BF)
-
-    def halo_body(i, _):
-        h_ext[i] = features(clips_halo[i])
-        return 0
-
-    lax.fori_loop(0, 4, halo_body, 0)
-    for k in range(3):
-        for i in range(10):
-            taps[k, i] = masked(live(k, i - 2), h_ext[i + 2 - k])
-
     def core_copy(g, k):
         return remote(
             core_out.at[g, k], core_in.at[g, k], core_send.at[g, k], core_recv.at[g, k], sibling
@@ -368,13 +354,13 @@
             line(h, d),
         )
 
-    def inner_copy(g, h, d):
+    def inner_copy(g, k, h, d):
         i = 3 * h + d - 1
         return remote(
-            inner_out.at[g, i],
-            inner_in.at[g, i],
-            inner_send.at[g, i],
-            inner_recv.at[g, i],
+            inner_out.at[g, k, i],
+            inner_in.at[g, k, i],
+            inner_send.at[g, k, i],
+            inner_recv.at[g, k, i],
             line(1 - h, d),
         )
 
@@ -391,23 +377,22 @@
             outer_out[g, k, 3 * h + d - 1] = block.astype(BF)
             outer_copy(g, k, h, d).start()
 
-    def inner_start(g):
-        for k in range(3):
-            for h, d in order:
-                outer_copy(g, k, h, d).wait_recv()
-            for h in range(2):
-                ref = acc.at[g, k, x] if h == 0 else acc.at[g, k, :, y]
-                total = ref[:, :, lanes(h)]
-                for d in range(1, 4):
-                    total = total + outer_in[g, k, 3 * h + d - 1].astype(F32)
-                ref[:, :, lanes(h)] = total
+    def inner_start(g, k):
+        for h, d in order:
+            outer_copy(g, k, h, d).wait_recv()
+        for h in range(2):
+            ref = acc.at[g, k, x] if h == 0 else acc.at[g, k, :, y]
+            total = ref[:, :, lanes(h)]
+            for d in range(1, 4):
+                total = total + outer_in[g, k, 3 * h + d - 1].astype(F32)
+            ref[:, :, lanes(h)] = total
         for h, d in order:
             if h == 0:
-                block = acc[g, :, x, (y + d) % 4, :, lanes(h)]
+                block = acc[g, k, x, (y + d) % 4, :, lanes(h)]
             else:
-                block = acc[g, :, (x + d) % 4, y, :, lanes(h)]
-            inner_out[g, 3 * h + d - 1] = block.astype(BF)
-            inner_copy(g, h, d).start()
+                block = acc[g, k, (x + d) % 4, y, :, lanes(h)]
+            inner_out[g, k, 3 * h + d - 1] = block.astype(BF)
+            inner_copy(g, k, h, d).start()
 
     def z_copy(g, d):
         return remote(
@@ -419,17 +404,18 @@
         )
 
     def z_start(g):
-        for h, d in order:
-            inner_copy(g, h, d).wait_recv()
-        for h in range(2):
-            total = acc[g, :, x, y, :, lanes(h)]
-            for d in range(1, 4):
-                total = total + inner_in[g, 3 * h + d - 1].astype(F32)
-            for r in range(2):
-                for q in range(2):
-                    part = total[:, r * 8 : r * 8 + 8, q * 128 : q * 128 + 128]
-                    z_wide[g, r * 4 + h * 2 + q] = part
-                    z_out[g, r * 4 + h * 2 + q] = part.astype(BF)
+        for k in range(3):
+            for h, d in order:
+                inner_copy(g, k, h, d).wait_recv()
+            for h in range(2):
+                total = acc[g, k, x, y, :, lanes(h)]
+                for d in range(1, 4):
+                    total = total + inner_in[g, k, 3 * h + d - 1].astype(F32)
+                for r in range(2):
+                    for q in range(2):
+                        part = total[r * 8 : r * 8 + 8, q * 128 : q * 128 + 128]
+                        z_wide[g, r * 4 + h * 2 + q, k] = part
+                        z_out[g, r * 4 + h * 2 + q, k] = part.astype(BF)
         for d in (4, 3, 5, 2, 6, 1, 7):
             z_copy(g, d).start()
 
@@ -456,11 +442,31 @@
         pieces[g, z, xl] = piece[g]
 
     def time_grad(k):
-        left = taps[k, pl.ds(2, FD)].reshape(FD * S, C)
+        left = h_ext[pl.ds(4, FD)] if k == 0 else taps[k, pl.ds(2, FD)]
+        left = left.reshape(FD * S, C)
         contribute(0, k, dot(left, gm[pl.ds(0, FD)].reshape(FD * S, C), 0, 0))
 
     time_grad(0)
     arrive_z(1, 4, 5, 6)
+
+    @pl.when(t > 0)
+    def _():
+        for f in range(4):
+            clips_copy(f, after).wait_recv()
+
+    @pl.when(t == 0)
+    def _():
+        clips_halo[...] = jnp.zeros((4, S, C), BF)
+
+    def halo_body(i, _):
+        h_ext[i] = features(clips_halo[i])
+        return 0
+
+    lax.fori_loop(0, 4, halo_body, 0)
+    for k in range(3):
+        for i in range(10):
+            taps[k, i] = masked(live(k, i - 2), h_ext[i + 2 - k])
+
     time_grad(1)
     reduce_tap(0, 0)
     time_grad(2)
@@ -471,19 +477,15 @@
     reduce_tap(0, 2)
     finish_weights(1)
 
-    def hidden_pair(i, wide):
-        total = wide
+    def hidden_three(i, wide):
+        total = wide.astype(F32).reshape(3 * S, C)
         for k in range(3):
-            total = total + dot(taps[k, pl.ds(i, 2)].reshape(2 * S, C), wt[k], 1, 0)
-        hid[pl.ds(i, 2)] = total.astype(BF).reshape(2, S, C)
-
-    hidden_pair(0, clips_halo[pl.ds(2, 2)].astype(F32).reshape(2 * S, C))
-
-    def hidden_body(i, _):
-        hidden_pair(2 + 2 * i, clips[pl.ds(2 * i, 2)].astype(F32).reshape(2 * S, C))
-        return 0
-
-    lax.fori_loop(0, FD // 2, hidden_body, 0)
+            total = total + dot(taps[k, pl.ds(i, 3)].reshape(3 * S, C), wt[k], 1, 0)
+        hid[pl.ds(i, 3)] = total.astype(BF).reshape(3, S, C)
+
+    hidden_three(0, jnp.concatenate([clips_halo[pl.ds(2, 2)], clips[pl.ds(0, 1)]], axis=0))
+    hidden_three(3, clips[pl.ds(1, 3)])
+    hidden_three(6, clips[pl.ds(4, 3)])
     for k in range(3):
         for j in range(HD):
             dtaps[k, j] = masked(live(k, 2 * j), hid[2 * j + 2 - k])
@@ -495,13 +497,15 @@
     down_grad(1)
     down_grad(2)
     reduce_tap(1, 0)
+    reduce_tap(1, 1)
+    inner_start(0, 0)
+    reduce_tap(1, 2)
+    inner_start(0, 1)
+    inner_start(0, 2)
     total = dot(dtaps[0].reshape(HD * S, C), wd[0], 1, 0)
     total = total + dot(dtaps[1].reshape(HD * S, C), wd[1], 1, 0)
-    reduce_tap(1, 1)
     total = total + dot(dtaps[2].reshape(HD * S, C), wd[2], 1, 0)
     reduced[...] = total.astype(BF).reshape(HD, S, C)
-    reduce_tap(1, 2)
-    inner_start(0)
 
     def clips_pair(i, _):
         here = pl.ds(2 * i, 2)
@@ -518,14 +522,17 @@
         grad_clips[here] = (gh[here].reshape(2 * S, C) + grad).astype(BF).reshape(2, S, C)
         return 0
 
-    lax.fori_loop(0, 2, clips_pair, 0)
     z_start(0)
+    inner_start(1, 0)
+    lax.fori_loop(0, 1, clips_pair, 0)
+    inner_start(1, 1)
+    inner_start(1, 2)
+    lax.fori_loop(1, 2, clips_pair, 0)
+    z_start(1)
+    piece_start(0)
     lax.fori_loop(2, 3, clips_pair, 0)
-    inner_start(1)
+    piece_start(1)
     lax.fori_loop(3, 4, clips_pair, 0)
-    piece_start(0)
-    z_start(1)
-    piece_start(1)
     for g in range(2):
         for other, d in sends:
             piece_copy(g, other, d).wait()
@@ -553,7 +560,7 @@
         for h, d in order:
             for k in range(3):
                 outer_copy(g, k, h, d).wait_send()
-            inner_copy(g, h, d).wait_send()
+                inner_copy(g, k, h, d).wait_send()
         for d in range(1, NZ):
             z_copy(g, d).wait_send()
 
@@ -583,7 +590,7 @@
             pltpu.VMEM((3, FD + 2, S, C), BF),
             pltpu.VMEM((FD + 2, S, C), F32),
             pltpu.VMEM((FD + 2, S, C), BF),
-            pltpu.VMEM((FD + 2, S, C), BF),
+            pltpu.VMEM((FD + 1, S, C), BF),
             pltpu.VMEM((3, HD, S, C), BF),
             pltpu.VMEM((2, FD, S, C), BF),
             pltpu.VMEM((2, 4, 2, 2, 2, 16, C), F32),
@@ -592,22 +599,22 @@
             pltpu.VMEM((2, 3, 4, 4, 16, C), BF),
             pltpu.VMEM((2, 3, 6, 4, 16, C // 2), BF),
             pltpu.VMEM((2, 3, 6, 4, 16, C // 2), BF),
-            pltpu.VMEM((2, 6, 3, 16, C // 2), BF),
-            pltpu.VMEM((2, 6, 3, 16, C // 2), BF),
+            pltpu.VMEM((2, 3, 6, 16, C // 2), BF),
+            pltpu.VMEM((2, 3, 6, 16, C // 2), BF),
             pltpu.VMEM((2, NZ, 3, 8, 128), F32),
             pltpu.VMEM((2, NZ, 3, 8, 128), BF),
             pltpu.VMEM((2, NZ - 1, 3, 8, 128), BF),
             pltpu.VMEM((2, 3, 8, 128), BF),
-            dma((2, 36)),
-            dma((2, 36)),
+            dma((2, 43)),
+            dma((2, 43)),
             dma((6,)),
             dma((6,)),
             dma((2, 3)),
             dma((2, 3)),
             dma((2, 3, 6)),
             dma((2, 3, 6)),
-            dma((2, 6)),
-            dma((2, 6)),
+            dma((2, 3, 6)),
+            dma((2, 3, 6)),
             dma((2, NZ - 1)),
             dma((2, NZ - 1)),
             dma((2, 2 * NZ)),

time: 69.9 us -> 66.2 us (0.947)
  Pallas kernels: 69.1 us -> 65.3 us
    pallas_call x1, Pallas kernels: 67.8 us -> 64 us  [shards(): pl.pallas_call(kernel, out_shape=(jax.ShapeDtypeStruct((HD, S, C), BF), j...]
where the time goes in v5:
time: 66.2 us; the launch traced here: 66.1 us
  Pallas kernels  65.3 us (99%)
  between operations  0.8 us (1%)
    pallas_call x1, Pallas kernels, shards(): pl.pallas_call(kernel, out_shape=(jax.ShapeDtypeStruct((HD, S, C), BF), j...  64 us

profile of v5, /device:TPU:2, one launch (start us, length us, event | category | flops | bytes accessed | tf_op | source)
XLA Modules:
  0.0 66.1 jit_solution(11376290085799245259)
XLA Ops:
  0.6 64.0 %clip_conv.1 = (bf16[4,128,512]{2,1,0:T(8,128)(2,1)S(1)}, bf16[8,128,512]{2,1,0:T(8,128)(2,1)S(1)}, bf16[2,8,2,3,8,128]{5,4,3,2,1,0:T(8,128)(2,1)S(1)}) custom-call(s32[1,8]{1,0:T(1,128)} %lengths_in.1, bf16[8,128,512]{2,1,0:T(8,128)(2,1)} %bitcast.4, bf16[3,32,512]{2,1,0:T(8,128)(2,1)} %wt_own.1, bf16[3,32,512]{2,1,0:T(8,128)(2,1)} %wd_own.1, ...), custom_call_target="tpu_custom_call" | custom-call | tf_op jit(solution)/shard_map/clip_conv/pallas_call | solution.py:573
  64.6 1.3 %deliver.1 = (bf16[4,128,512]{2,1,0:T(8,128)(2,1)}, bf16[8,128,512]{2,1,0:T(8,128)(2,1)}, f32[3,32,512]{2,1,0:T(8,128)}, f32[3,32,512]{2,1,0:T(8,128)}) custom-call(bf16[4,128,512]{2,1,0:T(8,128)(2,1)S(1)} %get-tuple-element.11.reduced, bf16[8,128,512]{2,1,0:T(8,128)(2,1)S(1)} %get-tuple-element.12.grad_clips, ...), custom_call_target="tpu_custom_call" | custom-call | tf_op jit(solution)/shard_map/deliver/pallas_call | solution.py:629

commit v6 on v5

--- a/solution.py
+++ b/solution.py
@@ -524,15 +524,14 @@
 
     z_start(0)
     inner_start(1, 0)
-    lax.fori_loop(0, 1, clips_pair, 0)
     inner_start(1, 1)
     inner_start(1, 2)
-    lax.fori_loop(1, 2, clips_pair, 0)
+    lax.fori_loop(0, 1, clips_pair, 0)
     z_start(1)
     piece_start(0)
-    lax.fori_loop(2, 3, clips_pair, 0)
+    lax.fori_loop(1, 2, clips_pair, 0)
     piece_start(1)
-    lax.fori_loop(3, 4, clips_pair, 0)
+    lax.fori_loop(2, 4, clips_pair, 0)
     for g in range(2):
         for other, d in sends:
             piece_copy(g, other, d).wait()

time: 66.2 us -> 65.4 us (0.988)
  Pallas kernels: 65.3 us -> 64.5 us
    pallas_call x1, Pallas kernels: 64 us -> 63.2 us  [shards(): pl.pallas_call(kernel, out_shape=(jax.ShapeDtypeStruct((HD, S, C), BF), j...]
where the time goes in v6:
time: 65.4 us; the launch traced here: 65.3 us
  Pallas kernels  64.5 us (99%)
  between operations  0.8 us (1%)
    pallas_call x1, Pallas kernels, shards(): pl.pallas_call(kernel, out_shape=(jax.ShapeDtypeStruct((HD, S, C), BF), j...  63.2 us

profile of v6, /device:TPU:2, one launch (start us, length us, event | category | flops | bytes accessed | tf_op | source)
XLA Modules:
  0.0 65.3 jit_solution(12234782924606810551)
XLA Ops:
  0.6 63.2 %clip_conv.1 = (bf16[4,128,512]{2,1,0:T(8,128)(2,1)S(1)}, bf16[8,128,512]{2,1,0:T(8,128)(2,1)S(1)}, bf16[2,8,2,3,8,128]{5,4,3,2,1,0:T(8,128)(2,1)S(1)}) custom-call(s32[1,8]{1,0:T(1,128)} %lengths_in.1, bf16[8,128,512]{2,1,0:T(8,128)(2,1)} %bitcast.4, bf16[3,32,512]{2,1,0:T(8,128)(2,1)} %wt_own.1, bf16[3,32,512]{2,1,0:T(8,128)(2,1)} %wd_own.1, ...), custom_call_target="tpu_custom_call" | custom-call | tf_op jit(solution)/shard_map/clip_conv/pallas_call | solution.py:572
  63.8 1.3 %deliver.1 = (bf16[4,128,512]{2,1,0:T(8,128)(2,1)}, bf16[8,128,512]{2,1,0:T(8,128)(2,1)}, f32[3,32,512]{2,1,0:T(8,128)}, f32[3,32,512]{2,1,0:T(8,128)}) custom-call(bf16[4,128,512]{2,1,0:T(8,128)(2,1)S(1)} %get-tuple-element.11.reduced, bf16[8,128,512]{2,1,0:T(8,128)(2,1)S(1)} %get-tuple-element.12.grad_clips, ...), custom_call_target="tpu_custom_call" | custom-call | tf_op jit(solution)/shard_map/deliver/pallas_call | solution.py:628
